TPU v7x, 512 devices: a whole 4x8x8 slice. The times are simulated.
512 devices in a mesh: ctx: 16 (over y, x_lo), exp: 32 (over x_hi, z, core).
Axes of the slice: x: 4 (x_hi: 2, x_lo: 2; x = x_hi * 2 + x_lo), y: 8, z: 8, core: 2. Of those that a mesh axis runs over, the one named last changes fastest.
Arguments:
- queries: bfloat16 [32, 1024, 2048], P('exp', 'ctx'), may hold values from -21 to 21
- keys: bfloat16 [32, 1024, 256], P('exp', 'ctx'), may hold values from -6 to 6
- values: bfloat16 [32, 1024, 256], P('exp', 'ctx'), may hold values from -4 to 4
- sinks: float32 [32], replicated, may hold values from -1 to 3
- out_weight: bfloat16 [2048, 1440], P('exp'), may hold values from -0.125 to 0.125
- norm_gain: float32 [1440], replicated, may hold values from 0.1 to 1.9
- routes: int32 [32, 1024, 4], P('exp', 'ctx'), may hold values from 0 to 15, all different within a row; in each aligned block of 64 rows (0 to 63, 64 to 127, ..., all dimensions but the last counted through in order) at most 20 rows name the same one
- gates: float32 [32, 1024, 4], P('exp', 'ctx'), may hold values from 0.1 to 1
- gate_codes: int32 [32, 1440, 192], P('exp'), may hold values from 0 to 65535, as said below
- up_codes: int32 [32, 1440, 192], P('exp'), may hold values from 0 to 65535, as said below
- down_codes: int32 [32, 768, 360], P('exp'), may hold values from 0 to 65535, as said below
- gate_scales: int32 [32, 45, 768], P('exp'), may hold values from 118 to 121
- up_scales: int32 [32, 45, 768], P('exp'), may hold values from 118 to 121
- down_scales: int32 [32, 24, 1440], P('exp'), may hold values from 118 to 121
Outputs:
- layer_out: bfloat16 [32, 1024, 1440], P('exp', 'ctx')
Inputs may be any that keep to these rules, and one draw needn't show every extreme that they name: `routes`: each token names 4 different experts; within the tokens of one device (aligned blocks of 64 rows) no expert is named by more than 20 tokens, a bound that some block reaches. `gate_codes`: each word packs four 4-bit codes; code k lies in bits 4k to 4k+3 and belongs to hidden unit 4q+k of word column q. `up_codes`: each word packs four 4-bit codes; code k lies in bits 4k to 4k+3 and belongs to hidden unit 4q+k of word column q. `down_codes`: each word packs four 4-bit codes; code k lies in bits 4k to 4k+3 and belongs to feature 4q+k of word column q.
All inputs are finite; a program needn't handle non-finite values.
Results may differ from a plain program's by a relative error of at most 0.023.
Values may be sent and summed in bfloat16 or wider, within the bound.
A program may use at most 128 MiB of HBM per device.

v0:
```python
import math

import jax
import jax.numpy as jnp
from jax import lax
from jax.sharding import PartitionSpec as P

QH = 32
KVH = 4
HD = 64
TOPK = 4
SPLIT = 2


def decode_block(codes, scales):
    shifts = jnp.array([0, 4, 8, 12], dtype=jnp.int32)
    nibble = jnp.right_shift(codes[..., None], shifts) & 15
    nibble = nibble.reshape(codes.shape[0], codes.shape[1] * 4)
    magnitude = nibble & 7
    mag_float = magnitude.astype(jnp.float32)
    levels = jnp.where(
        magnitude < 2,
        0.5 * mag_float,
        jnp.exp2(jnp.right_shift(magnitude, 1).astype(jnp.float32) - 1.0)
        * (1.0 + 0.5 * (magnitude & 1).astype(jnp.float32)),
    )
    signed = jnp.where(nibble >= 8, -levels, levels)
    factor = jnp.exp2(jnp.repeat(scales, 32, axis=0).astype(jnp.float32) - 127.0)
    return (signed * factor).astype(jnp.bfloat16)


def expert_rows(slot_rows, w_gate, w_up, w_down):
    flat_rows = slot_rows.reshape(-1, slot_rows.shape[-1])
    gate_act = jnp.dot(flat_rows, w_gate, preferred_element_type=jnp.float32)
    up_act = jnp.dot(flat_rows, w_up, preferred_element_type=jnp.float32)
    active = ((up_act + 1.0) * gate_act * jax.nn.sigmoid(1.702 * gate_act)).astype(jnp.bfloat16)
    result = jnp.dot(active, w_down, preferred_element_type=jnp.float32).astype(jnp.bfloat16)
    return result.reshape(slot_rows.shape)


def attend(local_queries, offset, key_all, value_all, sinks):
    row_count = local_queries.shape[0]
    groups = QH // KVH
    scale = 1.0 / math.sqrt(HD)
    grouped = local_queries.reshape(row_count, KVH, groups, HD)
    key_heads = key_all.reshape(-1, KVH, HD)
    value_heads = value_all.reshape(-1, KVH, HD)
    key_span = 128
    positions = offset + jnp.arange(row_count, dtype=jnp.int32)
    sink_init = jnp.broadcast_to(sinks.reshape(KVH, 1, groups), (KVH, row_count, groups))
    start_state = (
        sink_init,
        jnp.ones_like(sink_init),
        jnp.zeros((KVH, row_count, groups, HD), jnp.float32),
    )

    def advance(block_index, carry):
        run_max, total_sum, numerator = carry
        key_start = block_index * key_span
        key_block = lax.dynamic_slice_in_dim(key_heads, key_start, key_span, 0)
        value_block = lax.dynamic_slice_in_dim(value_heads, key_start, key_span, 0)
        scores = (
            jnp.einsum("nhsd,khd->hnsk", grouped, key_block, preferred_element_type=jnp.float32)
            * scale
        )
        key_pos = key_start + jnp.arange(key_span, dtype=jnp.int32)
        allowed = key_pos[None, None, None, :] <= positions[None, :, None, None]
        scores = jnp.where(allowed, scores, -1e30)
        new_max = jnp.maximum(run_max, jnp.max(scores, axis=-1))
        weights = jnp.exp(scores - new_max[..., None])
        shrink = jnp.exp(run_max - new_max)
        total_sum = total_sum * shrink + jnp.sum(weights, axis=-1)
        numerator = numerator * shrink[..., None] + jnp.einsum(
            "hnsk,khd->hnsd",
            weights.astype(jnp.bfloat16),
            value_block,
            preferred_element_type=jnp.float32,
        )
        return (new_max, total_sum, numerator)

    blocks = (offset + row_count + key_span - 1) // key_span
    run_max, total_sum, numerator = lax.fori_loop(0, blocks, advance, start_state)
    result = numerator / total_sum[..., None]
    return jnp.transpose(result, (1, 0, 2, 3)).reshape(row_count, QH * HD).astype(jnp.bfloat16)


def local(
    queries,
    keys,
    values,
    sinks,
    out_weight,
    norm_gain,
    routes,
    gates,
    gate_codes,
    up_codes,
    down_codes,
    gate_scales,
    up_scales,
    down_scales,
):
    tokens = queries.shape[1]
    ctx_rank = lax.axis_index("ctx")
    key_all, value_all = (
        lax.all_gather(keys[0], "ctx", axis=0, tiled=True),
        lax.all_gather(values[0], "ctx", axis=0, tiled=True),
    )
    local_q = queries[0]
    attended = attend(local_q, ctx_rank * tokens, key_all, value_all, sinks)
    width = out_weight.shape[1]
    branch = jnp.dot(
        attended,
        lax.all_gather(out_weight, "exp", axis=0, tiled=True),
        preferred_element_type=jnp.float32,
    )
    mean_sq = jnp.mean(branch * branch, axis=-1, keepdims=True)
    normed = (branch * lax.rsqrt(mean_sq + 1e-05) * norm_gain).astype(jnp.bfloat16)
    slices = lax.axis_size("exp")
    experts = slices // SPLIT
    capacity = min(tokens, 2 * max(1, tokens * TOPK * 5 // (8 * experts)))
    route_ids = routes[0].reshape(-1)
    hit_table = (route_ids[:, None] == jnp.arange(experts, dtype=jnp.int32)[None, :]).astype(
        jnp.int32
    )
    slot_order = jnp.sum((jnp.cumsum(hit_table, axis=0) - 1) * hit_table, axis=1)
    target = route_ids * capacity + slot_order
    placed = jnp.arange(experts * capacity, dtype=jnp.int32)[:, None] == target[None, :]
    dispatch = jnp.any(placed.reshape(experts * capacity, tokens, TOPK), axis=2).astype(
        jnp.bfloat16
    )
    combine = jnp.sum(
        jnp.where(placed, gates[0].reshape(1, -1), 0.0).reshape(experts * capacity, tokens, TOPK),
        axis=2,
    ).T
    buffer = (
        jnp.dot(dispatch, normed, preferred_element_type=jnp.float32)
        .astype(jnp.bfloat16)
        .reshape(experts, capacity, width)
    )
    w_gate = decode_block(gate_codes[0], gate_scales[0])
    w_up = decode_block(up_codes[0], up_scales[0])
    w_down = decode_block(down_codes[0], down_scales[0])
    outgoing = jnp.broadcast_to(buffer[:, None], (experts, SPLIT, capacity, width)).reshape(
        slices, capacity, width
    )
    partial_value = expert_rows(
        lax.all_to_all(outgoing, "exp", split_axis=0, concat_axis=0, tiled=True),
        w_gate,
        w_up,
        w_down,
    )
    returned = lax.all_to_all(partial_value, "exp", split_axis=0, concat_axis=0, tiled=True)
    pieces = returned.reshape(experts, SPLIT, capacity, width).astype(jnp.float32)
    expert_out = jnp.sum(pieces, axis=1).astype(jnp.bfloat16)
    mixed = jnp.dot(
        combine,
        expert_out.reshape(experts * capacity, width).astype(jnp.float32),
        precision=lax.Precision.HIGHEST,
    )
    return (branch + mixed).astype(jnp.bfloat16)[None]


def solution(mesh):
    return jax.shard_map(
        local,
        mesh=mesh,
        in_specs=(
            P("exp", "ctx", None),
            P("exp", "ctx", None),
            P("exp", "ctx", None),
            P(),
            P("exp", None),
            P(),
            P("exp", "ctx", None),
            P("exp", "ctx", None),
            P("exp", None, None),
            P("exp", None, None),
            P("exp", None, None),
            P("exp", None, None),
            P("exp", None, None),
            P("exp", None, None),
        ),
        out_specs=P("exp", "ctx", None),
        check_vma=False,
    )
```

profile of v0, /device:TPU:122, one launch (start us, length us, event | category | flops | bytes accessed | tf_op | source)
XLA Modules:
  0.0 318.7 jit_solution(16159958319802893854)
XLA Ops:
  6.5 0.7 all-gather.4.cloned.1.call-update
  7.3 0.8 copy.67
  8.3 32.3 %all-gather = bf16[1,1024,256]{2,1,0:T(8,128)(2,1)S(1)} all-gather(bf16[1,64,256]{2,1,0:T(8,128)(2,1)} %param.20), channel_id=2, replica_groups=mesh['ctx'=16,'exp'=32] {'ctx'}, dimensions={1}, use_global_device_ids=true | all-gather | bytes 557056 | tf_op jit(solution)/shard_map/all_gather | solution.py:106
  40.7 36.7 %all-gather.1 = bf16[1,1024,256]{2,1,0:T(8,128)(2,1)S(1)} all-gather(bf16[1,64,256]{2,1,0:T(8,128)(2,1)} %param.21), channel_id=3, replica_groups=mesh['ctx'=16,'exp'=32] {'ctx'}, dimensions={1}, use_global_device_ids=true | all-gather | bytes 557056 | tf_op jit(solution)/shard_map/all_gather | solution.py:107
  77.7 1.5 reshape_squeeze.2
  79.6 16.4 %while.15 = (s32[]{:T(128)}, f32[4,64,8]{1,2,0:T(8,128)S(1)}, f32[4,64,8]{1,2,0:T(8,128)S(1)}, f32[4,64,8,64]{3,2,1,0:T(8,128)S(1)}, s32[]{:T(128)}, /*index=5*/...) while((s32[]{:T(128)}, f32[4,64,8]{1,2,0:T(8,128)S(1)}, ...), condition=%wide.region_3.4_spmd.clone, body=%wide.region_0.3_spmd.clone.sunk | while | flops 68956352 | bytes 5654203 | solution.py:82
  88.4 0.7 fusion.66
  98.6 7.1 %broadcast_in_dim.80 = f32[45,32,768]{1,0,2:T(8,128)} broadcast(f32[45,768]{0,1:T(8,128)S(1)} %bitcast.80), dimensions={0,2} | broadcast | bytes 4561920 | tf_op jit(solution)/shard_map/broadcast_in_dim | solution.py:28
  105.6 14.8 %exp2.124 = f32[1440,192,4]{0,2,1:T(4,128)} reshape(f32[45,32,768]{1,0,2:T(8,128)} %broadcast_in_dim.80) | data formatting | bytes 8847360 | tf_op jit(solution)/shard_map/exp2 | solution.py:28
  120.8 7.1 %broadcast_in_dim.81 = f32[45,32,768]{1,0,2:T(8,128)} broadcast(f32[45,768]{0,1:T(8,128)S(1)} %bitcast.81), dimensions={0,2} | broadcast | bytes 4561920 | tf_op jit(solution)/shard_map/broadcast_in_dim | solution.py:28
  127.9 14.3 %exp2.130 = f32[1440,192,4]{0,2,1:T(4,128)} reshape(f32[45,32,768]{1,0,2:T(8,128)} %broadcast_in_dim.81) | data formatting | bytes 8847360 | tf_op jit(solution)/shard_map/exp2 | solution.py:28
  142.3 4.1 %multiply_reduce_fusion = (f32[64]{0:T(128)S(1)}, f32[64,1440]{1,0:T(8,128)S(1)}) fusion(bf16[64,2048]{1,0:T(8,128)(2,1)S(1)} %convert_element_type.166, bf16[2048,1440]{1,0:T(8,128)(2,1)} %all-gather.4.cloned.1.call-done), kind=kOutput, calls=%fused_computation.48 | convolution fusion | flops 377671616 | bytes 6529280 | tf_op jit(solution)/shard_map/dot_general | solution.py:112
  146.4 0.8 copy-done
  148.0 1.6 broadcast_in_dim.79
  149.6 12.1 %all-to-all-start = ((bf16[32,20,1440]{2,1,0:T(8,128)(2,1)}), bf16[32,20,1440]{2,1,0:T(8,128)(2,1)}, u32[]{:S(2)}, u32[]{:S(2)}) async-start(bf16[32,20,1440]{2,1,0:T(8,128)(2,1)} %bitcast.6), calls=%async_computation | async-start | bytes 4718592 | tf_op jit(solution)/shard_map/all_to_all | solution.py:148
  161.7 16.7 %fusion.14 = (bf16[1440,192,4]{0,2,1:T(4,128)(2,1)S(1)}, bf16[1440,192,4]{0,2,1:T(4,128)(2,1)}) fusion(f32[1440,192,4]{0,2,1:T(4,128)} %exp2.124, s32[4]{0:T(128)S(1)} %iota_multiply_fusion, s32[1440,192]{0,1:T(8,128)S(1)} %bitcast.84, f32[1440,192,4]{0,2,1:T(4,128)} %exp2.130, s32[1440,192]{0,1:T(8,128)} %bitcast.85), kind=kLoop, calls=%fused_computation.24 | loop fusion | flops 46448640 | bytes 15482896 | tf_op jit(solution)/shard_map/convert_element_type | solution.py:29
  178.4 4.9 %convert_element_type.181 = bf16[1440,768]{0,1:T(8,128)(2,1)} reshape(bf16[1440,192,4]{0,2,1:T(4,128)(2,1)} %get-tuple-element.130) | data formatting | bytes 4423680 | tf_op jit(solution)/shard_map/convert_element_type | solution.py:29
  183.3 2.5 convert_element_type.175
  186.0 2.7 broadcast_in_dim.82
  188.8 6.0 %copy.74 = f32[768,1440]{0,1:T(8,128)} copy(f32[768,1440]{1,0:T(8,128)} %bitcast.79) | data formatting | bytes 8847360 | tf_op jit(solution)/shard_map/exp2 | solution.py:28
  194.8 2.9 shift_right_arithmetic.102
  197.7 6.0 %shift_right_arithmetic.103 = s32[768,1440]{0,1:T(8,128)} reshape(s32[768,360,4]{0,2,1:T(4,128)} %shift_right_arithmetic.102) | data formatting | bytes 8847360 | tf_op jit(solution)/shard_map/shift_right_arithmetic | solution.py:17
  203.7 16.6 %all-to-all-done = bf16[32,20,1440]{2,1,0:T(8,128)(2,1)} async-done(((bf16[32,20,1440]{2,1,0:T(8,128)(2,1)}), bf16[32,20,1440]{2,1,0:T(8,128)(2,1)}, u32[]{:S(2)}, u32[]{:S(2)}) %all-to-all-start) | async-done | bytes 1843232 | tf_op jit(solution)/shard_map/all_to_all | solution.py:148
  220.3 4.1 %reshape.257 = bf16[640,1440]{1,0:T(8,128)(2,1)} reshape(bf16[32,20,1440]{2,1,0:T(8,128)(2,1)} %all-to-all-done) | data formatting | bytes 3686400 | tf_op jit(solution)/shard_map/reshape | solution.py:33
  224.5 4.6 %fusion.46 = f32[640,768]{1,0:T(8,128)} fusion(bf16[640,1440]{1,0:T(8,128)(2,1)} %reshape.257, bf16[1440,768]{0,1:T(8,128)(2,1)S(1)} %copy-done.1), kind=kOutput, calls=%fused_computation.79 | convolution fusion | flops 1415577600 | bytes 6021120 | tf_op jit(solution)/shard_map/dot_general | solution.py:34
  229.0 12.7 %convolution_convert_fusion = bf16[640,1440]{0,1:T(8,128)(2,1)} fusion(f32[768,1440]{0,1:T(8,128)} %copy.74, s32[768,1440]{0,1:T(8,128)} %shift_right_arithmetic.103, s32[1440]{0:T(1024)S(1)} %shift_right_arithmetic.105, f32[640,768]{1,0:T(8,128)} %fusion.46, bf16[640,1440]{1,0:T(8,128)(2,1)} %reshape.257, bf16[1440,768]{0,1:T(8,128)(2,1)} %convert_element_type.175), kind=kOutput, calls=%fused_computation.38 | convolution fusion | flops 2859233280 | bytes 16717440 | tf_op jit(solution)/shard_map/dot_general | solution.py:37
  241.7 2.6 copy.75
  244.4 2.1 reshape.258
  246.5 3.8 %all-to-all-start.1 = ((bf16[32,20,1440]{2,1,0:T(8,128)(2,1)}), bf16[32,20,1440]{2,1,0:T(8,128)(2,1)S(1)}, u32[]{:S(2)}, u32[]{:S(2)}) async-start(bf16[32,20,1440]{2,1,0:T(8,128)(2,1)} %reshape.258), calls=%async_computation.1 | async-start | bytes 4718592 | tf_op jit(solution)/shard_map/all_to_all | solution.py:153
  250.3 0.8 select_reduce_fusion
  251.1 57.4 %all-to-all-done.1 = bf16[32,20,1440]{2,1,0:T(8,128)(2,1)S(1)} async-done(((bf16[32,20,1440]{2,1,0:T(8,128)(2,1)}), bf16[32,20,1440]{2,1,0:T(8,128)(2,1)S(1)}, u32[]{:S(2)}, u32[]{:S(2)}) %all-to-all-start.1) | async-done | bytes 1843232 | tf_op jit(solution)/shard_map/all_to_all | solution.py:153
  309.4 2.4 fusion.26
  (136 shorter events, 21.0 us)
Async XLA Ops:
  6.5 72.8 %copy-start.9 = (f32[32]{0:T(128)S(1)}, f32[32]{0:T(128)}, u32[]{:S(2)}) copy-start(f32[32]{0:T(128)} %param.22) | copy-start | bytes 388
  6.5 135.8 %all-gather.4.cloned.1.call-start = ((), (), s32[]{:S(2)}) async-start(), calls=%async_computation.2 | async-start | bytes 6488064 | tf_op jit(solution)/shard_map/all_gather | solution.py:114
  79.6 18.5 %copy-start.5 = (s32[1,45,768]{2,0,1:T(1,128)S(1)}, s32[1,45,768]{2,0,1:T(1,128)}, u32[]{:S(2)}) copy-start(s32[1,45,768]{2,0,1:T(1,128)} %param.31) | copy-start | bytes 414724
  105.6 14.8 %copy-start.6 = (s32[1,45,768]{2,0,1:T(1,128)S(1)}, s32[1,45,768]{2,0,1:T(1,128)}, u32[]{:S(2)}) copy-start(s32[1,45,768]{2,0,1:T(1,128)} %param.30) | copy-start | bytes 414724
  142.2 5.0 %copy-start.7 = (f32[1440]{0:T(1024)S(1)}, f32[1440]{0:T(1024)}, u32[]{:S(2)}) copy-start(f32[1440]{0:T(1024)} %param.24) | copy-start | bytes 17284
  146.4 0.8 copy-start
  148.0 13.7 %copy-start.2 = (s32[1,1440,192]{1,2,0:T(8,128)S(1)}, s32[1,1440,192]{1,2,0:T(8,128)}, u32[]{:S(2)}) copy-start(s32[1,1440,192]{1,2,0:T(8,128)} %param.28) | copy-start | bytes 3317764
  149.6 70.7 %all-to-all-start = ((bf16[32,20,1440]{2,1,0:T(8,128)(2,1)}), bf16[32,20,1440]{2,1,0:T(8,128)(2,1)}, u32[]{:S(2)}, u32[]{:S(2)}) async-start(bf16[32,20,1440]{2,1,0:T(8,128)(2,1)} %bitcast.6), calls=%async_computation | async-start | bytes 4718592 | tf_op jit(solution)/shard_map/all_to_all | solution.py:148
  178.4 7.6 %copy-start.4 = (s32[1,24,1440]{2,1,0:T(8,128)S(1)}, s32[1,24,1440]{2,1,0:T(8,128)}, u32[]{:S(2)}) copy-start(s32[1,24,1440]{2,1,0:T(8,128)} %param.32) | copy-start | bytes 414724
  188.8 6.0 %copy-start.3 = (s32[1,768,360]{1,2,0:T(8,128)S(1)}, s32[1,768,360]{1,2,0:T(8,128)}, u32[]{:S(2)}) copy-start(s32[1,768,360]{1,2,0:T(8,128)} %param.29) | copy-start | bytes 3317764
  197.7 26.8 %copy-start.1 = (bf16[1440,768]{0,1:T(8,128)(2,1)S(1)}, bf16[1440,768]{0,1:T(8,128)(2,1)}, u32[]{:S(2)}) copy-start(bf16[1440,768]{0,1:T(8,128)(2,1)} %convert_element_type.181) | copy-start | bytes 6635524
  244.3 6.0 %copy-start.8 = (f32[1,64,4]{1,2,0:T(4,128)S(1)}, f32[1,64,4]{1,2,0:T(4,128)}, u32[]{:S(2)}) copy-start(f32[1,64,4]{1,2,0:T(4,128)} %param.26) | copy-start | bytes 3076
  246.5 62.0 %all-to-all-start.1 = ((bf16[32,20,1440]{2,1,0:T(8,128)(2,1)}), bf16[32,20,1440]{2,1,0:T(8,128)(2,1)S(1)}, u32[]{:S(2)}, u32[]{:S(2)}) async-start(bf16[32,20,1440]{2,1,0:T(8,128)(2,1)} %reshape.258), calls=%async_computation.1 | async-start | bytes 4718592 | tf_op jit(solution)/shard_map/all_to_all | solution.py:153
Sparse Core Ops, SparseCore 0:
  10.7 103.7 all-gather.3
where the time goes:
time: 320 us; the launch traced here: 319 us
  local copies, waits for them, and re-layouts  85.9 us (27%)
  waiting for transfers between devices  74.7 us (23%)
  blocking collectives  69 us (22%)
  matrix products  33.1 us (10%)
  other arithmetic  25.6 us (8%)
  starting transfers between devices  15.9 us (5%)
  between operations  13.7 us (4%)
    all_to_all x1, waiting for transfers between devices, local(): lax.all_to_all(partial_value, 'exp', split_axis=0, concat_axis=0, tiled=T...  57.4 us
    all_gather x1, blocking collectives, local(): lax.all_gather(values[0], 'ctx', axis=0, tiled=True)  36.7 us
    exp2 x5, local copies, waits for them, and re-layouts, decode_block(): jnp.exp2(jnp.repeat(scales, 32, axis=0).astype(jnp.float32) - 127.0)  35.5 us
    all_gather x1, blocking collectives, local(): lax.all_gather(keys[0], 'ctx', axis=0, tiled=True)  32.3 us
    broadcast_in_dim x3, local copies, waits for them, and re-layouts, decode_block(): jnp.repeat(scales, 32, axis=0).astype(jnp.float32) - 127.0  16.9 us
    convert_element_type x1, other arithmetic, decode_block(): return (signed * factor).astype(jnp.bfloat16)  16.7 us
    all_to_all x1, waiting for transfers between devices, local(): lax.all_to_all(outgoing, 'exp', split_axis=0, concat_axis=0, tiled=True)  16.6 us
    dot_general x1, matrix products, expert_rows(): jnp.dot(active, w_down, preferred_element_type=jnp.float32)  12.7 us
  transfers between devices with their start and end apart: 3, of which 2 were waited for; matrix products, arithmetic and copies ran while one was open for 34% of the time, Pallas kernels for 0%

commit v1 on v0

v1 whole, which is shorter than its diff:
```python
import functools
import math

import jax
import jax.numpy as jnp
from jax import lax
from jax.experimental import pallas as pl
from jax.experimental.pallas import tpu as pltpu
from jax.sharding import PartitionSpec as P

QH = 32
KVH = 4
HD = 64
TOPK = 4
D = 1440
DP = 1536
FF = 768
TOK = 64
CHIPS = 16
BLK = 240
MESH = pl.DeviceIdType.MESH
F32 = jnp.float32
BF16 = jnp.bfloat16

OFFSETS = []
for step in range(8):
    half = (step + 1) // 2
    dz = half if step % 2 else -half
    OFFSETS += [(0, dz), (1, dz)]


def iota(shape, axis):
    return lax.broadcasted_iota(jnp.int32, shape, axis)


def dot(a, b):
    return jnp.dot(a, b, preferred_element_type=F32)


def offset_expert(i, x_hi, z):
    step = i >> 1
    half = (step + 1) >> 1
    dz = jnp.where((step & 1) == 1, half, -half)
    return ((x_hi + (i & 1)) & 1) * 8 + ((z + dz + 8) & 7)


def split3(x):
    hi = x.astype(BF16)
    rest = x - hi.astype(F32)
    mid = rest.astype(BF16)
    low = (rest - mid.astype(F32)).astype(BF16)
    return hi, mid, low


def fp4_plane(words, shift):
    code = (words >> shift) & 15
    size = code & 7
    twice = size + jnp.maximum(size - 4, 0) + 2 * jnp.maximum(size - 6, 0)
    return jnp.where(code >= 8, -twice, twice).astype(F32).astype(BF16)


def decode(codes_ref, scales_ref, planes_ref, perm_ref, out_ref, rows, words, m_rows):
    blocks = [(b, min(128, words - b)) for b in range(0, words, 128)]

    def planes_step(i, _):
        r = pl.multiple_of(i * 32, 32)
        for b, (lo, count) in enumerate(blocks):
            w = codes_ref[pl.ds(r, 32), lo : lo + count]
            if count == 128:
                for k in range(4):
                    planes_ref[pl.ds(r, 32), 512 * b + 128 * k : 512 * b + 128 * (k + 1)] = fp4_plane(w, 4 * k)
            elif count == 64:
                ww = jnp.concatenate([w, w], axis=1)
                high = (iota((32, 128), 1) >> 6) * 4
                for k in range(2):
                    planes_ref[pl.ds(r, 32), 512 * b + 128 * k : 512 * b + 128 * (k + 1)] = fp4_plane(ww, high + 8 * k)
            else:
                ww = jnp.concatenate([w, jnp.zeros((32, 128 - count), jnp.int32)], axis=1)
                for k in range(4):
                    planes_ref[pl.ds(r, 32), 512 * b + 128 * k : 512 * b + 128 * (k + 1)] = fp4_plane(ww, 4 * k)
        return 0

    lax.fori_loop(0, rows // 32, planes_step, 0)

    def product_step(i, _):
        r = pl.multiple_of(i * m_rows, 32)
        for b, (lo, count) in enumerate(blocks):
            if count == 64:
                value = dot(planes_ref[pl.ds(r, m_rows), 512 * b : 512 * b + 256], perm_ref[512:768, :256])
                width = 256
            else:
                value = dot(planes_ref[pl.ds(r, m_rows), 512 * b : 512 * b + 512], perm_ref[:512, :])
                width = 4 * count
            value = value[:, :width]
            scale = scales_ref[i, :, 512 * b : 512 * b + width]
            factor = (1 << (scale - 118)).astype(F32) * (2.0**-10)
            factor = jnp.broadcast_to(factor[:, None, :], (m_rows // 32, 32, width)).reshape(m_rows, width)
            out_ref[pl.ds(r, m_rows), 512 * b : 512 * b + width] = (value * factor).astype(BF16)
        return 0

    lax.fori_loop(0, rows // m_rows, product_step, 0)


def moe_kernel(
    branch_ref, normed_ref, routes_ref, gates_ref, routes_t_ref, gc_hbm, uc_hbm, dc_hbm, gs_hbm, us_hbm, ds_hbm,
    out_ref,
    gc, uc, dc, gs, us, ds, planes, perm, wg, wu, wd,
    send, mine, other, p_mine, p_other, p_in, result, ret,
    in_sem, send_sem, mine_sem, fwd_sem, other_sem, pout_sem, pin_sem, res_sem, ret_sem,
):
    me = lax.axis_index("exp")
    core = me & 1
    z = (me >> 1) & 7
    x_hi = me >> 4

    def peer(i):
        dx, dz = OFFSETS[i]
        return {"exp": (((x_hi + dx) & 1) * 8 + ((z + dz + 8) & 7)) * 2 + core}

    def source(i):
        dx, dz = OFFSETS[i]
        return {"exp": (((x_hi + dx) & 1) * 8 + ((z - dz + 8) & 7)) * 2 + core}

    partner = {"exp": me ^ 1}

    loads = []
    for n, (src, dst) in enumerate(((gc_hbm, gc), (uc_hbm, uc), (dc_hbm, dc), (gs_hbm, gs), (us_hbm, us), (ds_hbm, ds))):
        copy = pltpu.make_async_copy(src, dst, in_sem.at[n])
        copy.start()
        loads.append(copy)

    barrier = pltpu.get_barrier_semaphore()
    for i in range(1, CHIPS):
        pl.semaphore_signal(barrier, inc=1, device_id=peer(i), device_id_type=MESH)
    pl.semaphore_signal(barrier, inc=1, device_id=partner, device_id_type=MESH)

    routes_t = routes_t_ref[...]
    expert = offset_expert(iota((CHIPS, TOK), 0), x_hi, z)
    hit = jnp.zeros((CHIPS, TOK), F32)
    for k in range(TOPK):
        hit = hit + (routes_t[k : k + 1, :] == expert).astype(F32)
    before = (iota((TOK, 256), 0) < (iota((TOK, 256), 1) & 63)).astype(BF16)
    same = (iota((TOK, 256), 0) == (iota((TOK, 256), 1) & 63)).astype(BF16)
    hit16 = hit.astype(BF16)
    slot4 = dot(hit16, before)
    hit4 = dot(hit16, same)
    slot4 = jnp.where(hit4 > 0.5, slot4, -1000.0)
    slot_i = slot4.astype(jnp.int32)
    slot_main = slot_i[:, :TOK]
    pick = (jnp.broadcast_to(slot_main[:, None, :], (CHIPS, 16, TOK)) == iota((CHIPS, 16, TOK), 1)).astype(F32)
    pick = pick.astype(BF16).reshape(CHIPS * 16, TOK)
    rows = dot(pick, normed_ref[...]).astype(BF16)
    for j in range(12):
        send[:, 16 * j : 16 * j + 16, :] = rows[:, 128 * j : 128 * j + 128].reshape(CHIPS, 16, 128)
    tail_key = jnp.where(slot_i >= 16, slot_i - 16 + 4 * (iota((CHIPS, 256), 1) >> 6), -1)
    tail = (jnp.broadcast_to(tail_key[:, None, :], (CHIPS, 16, 256)) == iota((CHIPS, 16, 256), 1)).astype(F32)
    tail = tail.astype(BF16).reshape(CHIPS * 16, 256)
    for g in range(3):
        stacked = jnp.concatenate([normed_ref[:, 128 * (4 * g + j) : 128 * (4 * g + j + 1)] for j in range(4)], axis=0)
        send[:, 192 + 16 * g : 208 + 16 * g, :] = dot(tail, stacked).astype(BF16).reshape(CHIPS, 16, 128)

    pl.semaphore_wait(barrier, CHIPS)

    outgoing = []
    for i in range(1, CHIPS):
        copy = pltpu.make_async_remote_copy(
            src_ref=send.at[i], dst_ref=mine.at[i], send_sem=send_sem.at[i], recv_sem=mine_sem.at[i],
            device_id=peer(i), device_id_type=MESH)
        copy.start()
        outgoing.append(copy)

    def forward(i):
        copy = pltpu.make_async_remote_copy(
            src_ref=send.at[0] if i == 0 else mine.at[i], dst_ref=other.at[i],
            send_sem=fwd_sem.at[i], recv_sem=other_sem.at[i],
            device_id=partner, device_id_type=MESH)
        copy.start()
        return copy

    forwards = [forward(0)]

    expert_of = offset_expert(iota((TOK, CHIPS), 1), x_hi, z)
    routes = routes_ref[...]
    gates = gates_ref[...]
    hits = jnp.zeros((TOK, CHIPS), F32)
    for k in range(TOPK):
        hits = hits + (routes[:, k : k + 1] == expert_of).astype(F32)
    earlier = (iota((TOK, TOK), 1) < iota((TOK, TOK), 0)).astype(BF16)
    slots = jnp.where(hits > 0.5, dot(earlier, hits.astype(BF16)), 100.0)
    spread = (iota((CHIPS, 256), 0) == (iota((CHIPS, 256), 1) >> 4)).astype(BF16)
    slots = dot(slots.astype(BF16), spread).astype(jnp.int32)
    column_expert = offset_expert(iota((TOK, 256), 1) >> 4, x_hi, z)
    weight = jnp.zeros((TOK, 256), F32)
    for k in range(TOPK):
        weight = weight + jnp.where(routes[:, k : k + 1] == column_expert, gates[:, k : k + 1], 0.0)
    place = iota((TOK, 256), 1) & 15
    combine_main = jnp.concatenate(split3(jnp.where(slots == place, weight, 0.0)), axis=0)
    combine_tail = [
        jnp.concatenate(split3(jnp.where((slots - 16 == (place & 3)) & ((place >> 2) == j), weight, 0.0)), axis=0)
        for j in range(4)
    ]

    wide = iota((512, 512), 0)
    perm[:512, :] = (iota((512, 512), 1) == 4 * (wide & 127) + (wide >> 7)).astype(F32).astype(BF16)
    narrow = iota((256, 512), 0)
    perm[512:768, :] = (iota((256, 512), 1) == 4 * (narrow & 63) + (narrow >> 6)).astype(F32).astype(BF16)
    wg[D:, :] = jnp.zeros((DP - D, FF), BF16)
    wu[D:, :] = jnp.zeros((DP - D, FF), BF16)
    wd[:, D:] = jnp.zeros((FF, DP - D), BF16)
    for copy in loads:
        copy.wait()
    decode(gc, gs, planes, perm, wg, D, 192, 288)
    decode(uc, us, planes, perm, wu, D, 192, 288)
    decode(dc, ds, planes, perm, wd, FF, 360, 256)

    a, b = iota((128, 128), 0), iota((128, 128), 1)
    to_rows = (b == ((a >> 2) & 7) * 16 + (a >> 5) * 4 + (a & 3)).astype(F32).astype(BF16)
    to_block = (a == ((b >> 2) & 7) * 16 + (b >> 5) * 4 + (b & 3)).astype(F32).astype(BF16)

    sent_pieces = []
    sent_results = []

    def finish(c):
        sent_pieces[c].wait_recv()
        for i in range(4 * c, 4 * c + 4):
            total = (p_mine[i].astype(F32) + p_in[i].astype(F32)).astype(BF16)
            if i == 0:
                ret[0] = total
            else:
                result[i] = total
        for i in range(max(1, 4 * c), 4 * c + 4):
            copy = pltpu.make_async_remote_copy(
                src_ref=result.at[i], dst_ref=ret.at[i], send_sem=res_sem.at[i], recv_sem=ret_sem.at[i],
                device_id=source(i), device_id_type=MESH)
            copy.start()
            sent_results.append(copy)

    for c in range(4):
        for i in range(max(1, 4 * c), 4 * c + 4):
            outgoing[i - 1].wait_recv()
            forwards.append(forward(i))
        for i in range(4 * c, 4 * c + 4):
            forwards[i].wait_recv()
        if c == 0:
            mine[0] = send[0]

        def both(lo, hi):
            return jnp.concatenate(
                [mine[4 * c : 4 * c + 4, lo:hi, :].reshape(64, 128), other[4 * c : 4 * c + 4, lo:hi, :].reshape(64, 128)],
                axis=0)

        main = jnp.concatenate([both(16 * j, 16 * j + 16) for j in range(12)], axis=1)
        tails = []
        for g in range(3):
            moved = dot(to_rows, both(192 + 16 * g, 208 + 16 * g)).astype(BF16)
            tails += [moved[32 * j : 32 * j + 32, :] for j in range(4)]
        x = jnp.concatenate([main, jnp.concatenate(tails, axis=1)], axis=0)
        gate_act = dot(x, wg[...])
        up_act = dot(x, wu[...])
        active = ((up_act + 1.0) * gate_act * jax.nn.sigmoid(1.702 * gate_act)).astype(BF16)
        y = dot(active, wd[...]).astype(BF16)
        for j in range(12):
            tile = y[:128, 128 * j : 128 * j + 128]
            p_mine[4 * c : 4 * c + 4, 16 * j : 16 * j + 16, :] = tile[:64].reshape(4, 16, 128)
            p_other[4 * c : 4 * c + 4, 16 * j : 16 * j + 16, :] = tile[64:].reshape(4, 16, 128)
        for g in range(3):
            tiles = jnp.concatenate([y[128:, 128 * (4 * g + j) : 128 * (4 * g + j + 1)] for j in range(4)], axis=0)
            back = dot(to_block, tiles).astype(BF16)
            p_mine[4 * c : 4 * c + 4, 192 + 16 * g : 208 + 16 * g, :] = back[:64].reshape(4, 16, 128)
            p_other[4 * c : 4 * c + 4, 192 + 16 * g : 208 + 16 * g, :] = back[64:].reshape(4, 16, 128)
        copy = pltpu.make_async_remote_copy(
            src_ref=p_other.at[pl.ds(4 * c, 4)], dst_ref=p_in.at[pl.ds(4 * c, 4)],
            send_sem=pout_sem.at[c], recv_sem=pin_sem.at[c], device_id=partner, device_id_type=MESH)
        copy.start()
        sent_pieces.append(copy)
        if c > 0:
            finish(c - 1)
    finish(3)

    for copy in sent_results:
        copy.wait_recv()
    for j in range(12):
        part = dot(combine_main, ret[:, 16 * j : 16 * j + 16, :].reshape(256, 128))
        g = j // 4
        part = part + dot(combine_tail[j % 4], ret[:, 192 + 16 * g : 208 + 16 * g, :].reshape(256, 128))
        mixed = part[:TOK] + part[TOK : 2 * TOK] + part[2 * TOK :]
        lo, hi = 128 * j, min(128 * j + 128, D)
        out_ref[:, lo:hi] = (branch_ref[:, lo:hi] + mixed[:, : hi - lo]).astype(BF16)

    for copy in outgoing + forwards + sent_pieces + sent_results:
        copy.wait_send()


def moe(branch, normed, routes, gates, gate_codes, up_codes, down_codes, gate_scales, up_scales, down_scales):
    vmem = pl.BlockSpec(memory_space=pltpu.VMEM)
    hbm = pl.BlockSpec(memory_space=pl.ANY)
    dma = pltpu.SemaphoreType.DMA
    blocks = pltpu.VMEM((CHIPS, BLK, 128), BF16)
    return pl.pallas_call(
        moe_kernel,
        out_shape=jax.ShapeDtypeStruct((TOK, D), BF16),
        in_specs=[vmem] * 5 + [hbm] * 6,
        out_specs=vmem,
        scratch_shapes=[
            pltpu.VMEM((D, 192), jnp.int32),
            pltpu.VMEM((D, 192), jnp.int32),
            pltpu.VMEM((FF, 360), jnp.int32),
            pltpu.VMEM((5, 9, FF), jnp.int32),
            pltpu.VMEM((5, 9, FF), jnp.int32),
            pltpu.VMEM((3, 8, D), jnp.int32),
            pltpu.VMEM((D, DP), BF16),
            pltpu.VMEM((FF, 512), BF16),
            pltpu.VMEM((DP, FF), BF16),
            pltpu.VMEM((DP, FF), BF16),
            pltpu.VMEM((FF, DP), BF16),
            blocks, blocks, blocks, blocks, blocks, blocks, blocks, blocks,
            dma((6,)), dma((CHIPS,)), dma((CHIPS,)), dma((CHIPS,)), dma((CHIPS,)), dma((4,)), dma((4,)),
            dma((CHIPS,)), dma((CHIPS,)),
        ],
        compiler_params=pltpu.CompilerParams(collective_id=0, has_side_effects=True, vmem_limit_bytes=60 * 1024 * 1024),
        name="experts",
    )(
        branch, normed, routes, gates, routes.T, gate_codes, up_codes, down_codes,
        gate_scales.reshape(5, 9, FF), up_scales.reshape(5, 9, FF), down_scales.reshape(3, 8, D),
    )


def attend(local_queries, offset, key_all, value_all, sinks):
    row_count = local_queries.shape[0]
    groups = QH // KVH
    scale = 1.0 / math.sqrt(HD)
    grouped = local_queries.reshape(row_count, KVH, groups, HD)
    key_heads = key_all.reshape(-1, KVH, HD)
    value_heads = value_all.reshape(-1, KVH, HD)
    key_span = 128
    positions = offset + jnp.arange(row_count, dtype=jnp.int32)
    sink_init = jnp.broadcast_to(sinks.reshape(KVH, 1, groups), (KVH, row_count, groups))
    start_state = (
        sink_init,
        jnp.ones_like(sink_init),
        jnp.zeros((KVH, row_count, groups, HD), jnp.float32),
    )

    def advance(block_index, carry):
        run_max, total_sum, numerator = carry
        key_start = block_index * key_span
        key_block = lax.dynamic_slice_in_dim(key_heads, key_start, key_span, 0)
        value_block = lax.dynamic_slice_in_dim(value_heads, key_start, key_span, 0)
        scores = (
            jnp.einsum("nhsd,khd->hnsk", grouped, key_block, preferred_element_type=jnp.float32)
            * scale
        )
        key_pos = key_start + jnp.arange(key_span, dtype=jnp.int32)
        allowed = key_pos[None, None, None, :] <= positions[None, :, None, None]
        scores = jnp.where(allowed, scores, -1e30)
        new_max = jnp.maximum(run_max, jnp.max(scores, axis=-1))
        weights = jnp.exp(scores - new_max[..., None])
        shrink = jnp.exp(run_max - new_max)
        total_sum = total_sum * shrink + jnp.sum(weights, axis=-1)
        numerator = numerator * shrink[..., None] + jnp.einsum(
            "hnsk,khd->hnsd",
            weights.astype(jnp.bfloat16),
            value_block,
            preferred_element_type=jnp.float32,
        )
        return (new_max, total_sum, numerator)

    blocks = (offset + row_count + key_span - 1) // key_span
    run_max, total_sum, numerator = lax.fori_loop(0, blocks, advance, start_state)
    result = numerator / total_sum[..., None]
    return jnp.transpose(result, (1, 0, 2, 3)).reshape(row_count, QH * HD).astype(jnp.bfloat16)


def local(
    queries,
    keys,
    values,
    sinks,
    out_weight,
    norm_gain,
    routes,
    gates,
    gate_codes,
    up_codes,
    down_codes,
    gate_scales,
    up_scales,
    down_scales,
):
    tokens = queries.shape[1]
    ctx_rank = lax.axis_index("ctx")
    key_all, value_all = (
        lax.all_gather(keys[0], "ctx", axis=0, tiled=True),
        lax.all_gather(values[0], "ctx", axis=0, tiled=True),
    )
    local_q = queries[0]
    attended = attend(local_q, ctx_rank * tokens, key_all, value_all, sinks)
    width = out_weight.shape[1]
    branch = jnp.dot(
        attended,
        lax.all_gather(out_weight, "exp", axis=0, tiled=True),
        preferred_element_type=jnp.float32,
    )
    mean_sq = jnp.mean(branch * branch, axis=-1, keepdims=True)
    normed = (branch * lax.rsqrt(mean_sq + 1e-05) * norm_gain).astype(jnp.bfloat16)
    normed = jnp.pad(normed, ((0, 0), (0, DP - D)))
    return moe(
        branch, normed, routes[0], gates[0], gate_codes[0], up_codes[0], down_codes[0],
        gate_scales[0], up_scales[0], down_scales[0],
    )[None]


def solution(mesh):
    return jax.shard_map(
        local,
        mesh=mesh,
        in_specs=(
            P("exp", "ctx", None),
            P("exp", "ctx", None),
            P("exp", "ctx", None),
            P(),
            P("exp", None),
            P(),
            P("exp", "ctx", None),
            P("exp", "ctx", None),
            P("exp", None, None),
            P("exp", None, None),
            P("exp", None, None),
            P("exp", None, None),
            P("exp", None, None),
            P("exp", None, None),
        ),
        out_specs=P("exp", "ctx", None),
        check_vma=False,
    )
```

time: 320 us -> 192 us (0.60)
  the two profiles are of different devices: /device:TPU:122 before, /device:TPU:1 now
where the time goes in v1:
time: 192 us; the launch traced here: 190 us
  Pallas kernels  58.1 us (30%)
  blocking collectives  58 us (30%)
  waiting for transfers between devices  41 us (21%)
  between operations  13.6 us (7%)
  local copies, waits for them, and re-layouts  12.4 us (6%)
  matrix products  5.17 us (3%)
    pallas_call x1, Pallas kernels, moe(): pl.pallas_call(moe_kernel, out_shape=jax.ShapeDtypeStruct((TOK, D), BF16)...  58.1 us
    all_gather x1, waiting for transfers between devices, local(): lax.all_gather(out_weight, 'exp', axis=0, tiled=True)  40.3 us
    all_gather x1, blocking collectives, local(): lax.all_gather(keys[0], 'ctx', axis=0, tiled=True)  31.5 us
    all_gather x1, blocking collectives, local(): lax.all_gather(values[0], 'ctx', axis=0, tiled=True)  26.6 us
    unnamed x30, local copies, waits for them, and re-layouts  7.63 us
    dot_general x1, matrix products, local(): jnp.dot(attended, lax.all_gather(out_weight, 'exp', axis=0, tiled=True),...  4.06 us
  transfers between devices with their start and end apart: 1, of which 1 were waited for; matrix products, arithmetic and copies ran while one was open for 7% of the time, Pallas kernels for 0%

profile of v1, /device:TPU:1, one launch (start us, length us, event | category | flops | bytes accessed | tf_op | source)
XLA Modules:
  0.0 190.2 jit_solution(6256089254955072301)
XLA Ops:
  6.5 0.7 all-gather.4.cloned.1.call-update
  7.3 31.5 %all-gather = bf16[1,1024,256]{2,1,0:T(8,128)(2,1)S(1)} all-gather(bf16[1,64,256]{2,1,0:T(8,128)(2,1)} %param.17), channel_id=2, replica_groups=mesh['ctx'=16,'exp'=32] {'ctx'}, dimensions={1}, use_global_device_ids=true | all-gather | bytes 557056 | tf_op jit(solution)/shard_map/all_gather | solution.py:393
  38.8 0.2 copy.27
  39.0 26.6 %all-gather.1 = bf16[1,1024,256]{2,1,0:T(8,128)(2,1)S(1)} all-gather(bf16[1,64,256]{2,1,0:T(8,128)(2,1)S(1)} %copy-done.7), channel_id=3, replica_groups=mesh['ctx'=16,'exp'=32] {'ctx'}, dimensions={1}, use_global_device_ids=true | all-gather | bytes 557056 | tf_op jit(solution)/shard_map/all_gather | solution.py:394
  65.5 0.2 copy.28
  65.8 0.5 reshape_squeeze.12
  66.3 0.2 copy.29
  66.7 2.0 %while.15 = (s32[]{:T(128)}, f32[4,64,8]{1,2,0:T(8,128)S(1)}, f32[4,64,8]{1,2,0:T(8,128)S(1)}, f32[4,64,8,64]{3,2,1,0:T(8,128)S(1)}, s32[]{:T(128)}, /*index=5*/...) while((s32[]{:T(128)}, f32[4,64,8]{1,2,0:T(8,128)S(1)}, ...), condition=%wide.region_3.4_spmd.clone, body=%wide.region_0.3_spmd.clone.sunk | while | flops 68956352 | bytes 5654203 | solution.py:369
  66.9 0.5 fusion.26
  67.4 0.6 fusion.27
  68.1 0.1 copy.46
  68.2 0.6 convolution_add_fusion.2
  68.9 0.3 fusion.13
  69.3 0.1 copy.31
  69.4 0.5 convert_element_type.19
  69.8 0.4 copy-done.1
  70.2 1.6 copy.33
  71.7 1.6 copy.34
  73.4 0.1 copy-done.3
  73.5 1.4 copy.35
  74.9 0.3 reduce
  75.2 0.7 reshape_squeeze.13.gs_hbm
  76.0 0.3 reduce.1
  76.3 0.7 reshape_squeeze.14.us_hbm
  77.0 0.7 copy.32
  77.7 0.7 copy.36.routes_ref
  78.4 40.3 %all-gather.4.cloned.1.call-done = bf16[2048,1440]{1,0:T(8,128)(2,1)} async-done(((bf16[64,1440]{1,0:T(8,128)(2,1)}), bf16[2048,1440]{1,0:T(8,128)(2,1)}) %all-gather.4.cloned.1.call-update) | async-done | bytes 5898256 | tf_op jit(solution)/shard_map/all_gather | solution.py:401
  118.7 4.1 %multiply_reduce_fusion = (f32[64]{0:T(128)S(1)}, f32[64,1440]{1,0:T(8,128)S(1)}) fusion(bf16[64,2048]{1,0:T(8,128)(2,1)S(1)} %convert_element_type.19, bf16[2048,1440]{1,0:T(8,128)(2,1)} %all-gather.4.cloned.1.call-done), kind=kOutput, calls=%fused_computation.23 | convolution fusion | flops 377671616 | bytes 6529280 | tf_op jit(solution)/shard_map/dot_general | solution.py:399
  122.8 0.1 multiply_convert_fusion
  122.9 0.7 pad.4.normed_ref
  123.6 58.1 %experts.1 = bf16[64,1440]{1,0:T(8,128)(2,1)} custom-call(f32[64,1440]{1,0:T(8,128)} %copy-done, bf16[64,1536]{1,0:T(8,128)(2,1)} %pad.4.normed_ref, s32[64,4]{1,0:T(8,128)} %copy.36.routes_ref, f32[64,4]{1,0:T(8,128)} %bitcast.47, s32[4,64]{1,0:T(4,128)} %bitcast.48, s32[1440,192]{1,0:T(8,128)} %bitcast.40, s32[1440,192]{1,0:T(8,128)} %bitcast.41, ...), custom_call_target="tpu_custom_call" | custom-call | tf_op jit(solution)/shard_map/experts/pallas_call | solution.py:299
  181.7 1.6 copy.60
  (35 shorter events, 0.5 us)
Async XLA Ops:
  6.5 32.4 %copy-start.7 = (bf16[1,64,256]{2,1,0:T(8,128)(2,1)S(1)}, bf16[1,64,256]{2,1,0:T(8,128)(2,1)}, u32[]{:S(2)}) copy-start(bf16[1,64,256]{2,1,0:T(8,128)(2,1)} %param.18) | copy-start | bytes 98308
  6.5 112.2 %all-gather.4.cloned.1.call-start = ((), (), s32[]{:S(2)}) async-start(), calls=%async_computation | async-start | bytes 6488064 | tf_op jit(solution)/shard_map/all_gather | solution.py:401
  7.3 58.5 %copy-start.4 = (bf16[1,64,2048]{2,1,0:T(8,128)(2,1)S(1)}, bf16[1,64,2048]{2,1,0:T(8,128)(2,1)}, u32[]{:S(2)}) copy-start(bf16[1,64,2048]{2,1,0:T(8,128)(2,1)} %param.16) | copy-start | bytes 786436
  65.5 1.0 copy-start.11
  68.9 1.3 copy-start.1
  70.2 1.6 copy-start.2
  71.7 1.8 copy-start.3
  73.5 1.4 copy-start.5
  73.5 2.5 %copy-start.6 = (s32[1,45,768]{2,0,1:T(1,128)S(1)}, s32[1,45,768]{2,0,1:T(1,128)}, u32[]{:S(2)}) copy-start(s32[1,45,768]{2,0,1:T(1,128)} %param.28) | copy-start | bytes 414724
  73.5 3.5 %copy-start.10 = (f32[1,64,4]{1,2,0:T(4,128)S(1)}, f32[1,64,4]{1,2,0:T(4,128)}, u32[]{:S(2)}) copy-start(f32[1,64,4]{1,2,0:T(4,128)} %param.23) | copy-start | bytes 3076
  73.5 4.2 %copy-start.8 = (s32[1,64,4]{1,2,0:T(4,128)S(1)}, s32[1,64,4]{1,2,0:T(4,128)}, u32[]{:S(2)}) copy-start(s32[1,64,4]{1,2,0:T(4,128)} %param.22) | copy-start | bytes 3076
  78.4 44.4 %copy-start.9 = (f32[1440]{0:T(1024)S(1)}, f32[1440]{0:T(1024)}, u32[]{:S(2)}) copy-start(f32[1440]{0:T(1024)} %param.21) | copy-start | bytes 17284
  122.8 0.8 copy-start
Sparse Core Ops, SparseCore 0:
  10.7 107.9 all-gather.3

commit v2 on v1

v2 whole, which is shorter than its diff:
```python
import functools
import math

import jax
import jax.numpy as jnp
from jax import lax
from jax.experimental import pallas as pl
from jax.experimental.pallas import tpu as pltpu
from jax.sharding import PartitionSpec as P

QH = 32
KVH = 4
HD = 64
TOPK = 4
D = 1440
DP = 1536
FF = 768
TOK = 64
CHIPS = 16
BLK = 240
MESH = pl.DeviceIdType.MESH
F32 = jnp.float32
BF16 = jnp.bfloat16

OFFSETS = []
for step in range(8):
    half = (step + 1) // 2
    dz = half if step % 2 else -half
    OFFSETS += [(0, dz), (1, dz)]


def iota(shape, axis):
    return lax.broadcasted_iota(jnp.int32, shape, axis)


def dot(a, b):
    return jnp.dot(a, b, preferred_element_type=F32)


def offset_expert(i, x_hi, z):
    step = i >> 1
    half = (step + 1) >> 1
    dz = jnp.where((step & 1) == 1, half, -half)
    return ((x_hi + (i & 1)) & 1) * 8 + ((z + dz + 8) & 7)


def split3(x):
    hi = x.astype(BF16)
    rest = x - hi.astype(F32)
    mid = rest.astype(BF16)
    low = (rest - mid.astype(F32)).astype(BF16)
    return hi, mid, low


def fp4_plane(words, shift):
    code = (words >> shift) & 15
    size = code & 7
    twice = size + jnp.maximum(size - 4, 0) + 2 * jnp.maximum(size - 6, 0)
    return jnp.where(code >= 8, -twice, twice).astype(F32).astype(BF16)


def turn(source_ref, target_ref, rows, words):
    for lo in range(0, rows, 128):
        hi = min(lo + 128, rows)
        target_ref[lo:hi, :] = jnp.transpose(source_ref[:, lo:hi])


def code_planes(codes_ref, planes_ref, rows, words):
    blocks = [(b, 128 * b, min(128, words - 128 * b)) for b in range((words + 127) // 128)]

    def step(i, _):
        r = pl.multiple_of(i * 32, 32)
        for b, lo, count in blocks:
            w = codes_ref[pl.ds(r, 32), lo : lo + count]
            if count == 64:
                w = jnp.concatenate([w, w], axis=1)
                shifts = [(iota((32, 128), 1) >> 6) * 4 + 8 * k for k in range(2)]
            else:
                if count < 128:
                    w = jnp.concatenate([w, jnp.zeros((32, 128 - count), jnp.int32)], axis=1)
                shifts = [4 * k for k in range(4)]
            for k, shift in enumerate(shifts):
                at = 512 * b + 128 * k
                planes_ref[pl.ds(r, 32), at : at + 128] = fp4_plane(w, shift)
        return 0

    lax.fori_loop(0, rows // 32, step, 0)


def weight_rows(planes_ref, scales_ref, perm_ref, out_ref, rows, words, m_rows):
    groups = m_rows // 32
    blocks = [(b, min(128, words - 128 * b)) for b in range((words + 127) // 128)]
    for i in range(rows // m_rows):
        r = i * m_rows
        for b, count in blocks:
            width = 4 * count
            if count == 64:
                value = dot(planes_ref[r : r + m_rows, 512 * b : 512 * b + 256], perm_ref[512:768, :256])
            else:
                value = dot(planes_ref[r : r + m_rows, 512 * b : 512 * b + 512], perm_ref[:512, :])
            value = value[:, :width]
            scale = scales_ref[groups * i : groups * (i + 1), 512 * b : 512 * b + width]
            factor = (1 << (scale - 118)).astype(F32) * (2.0**-10)
            for n in range(groups):
                piece = value[32 * n : 32 * n + 32] * factor[n : n + 1]
                out_ref[r + 32 * n : r + 32 * n + 32, 512 * b : 512 * b + width] = piece.astype(BF16)


class Gather:
    RELAYS = {
        ("A", 1): "+", ("A", 2): "+s", ("A", 3): "+s", ("A", 4): "s",
        ("A", -1): "-", ("A", -2): "-", ("A", -3): "s",
        ("B", 0): "+-", ("B", -1): "-",
    }

    def __init__(self, buf, index, sends, recvs, there, partner=None, share=None):
        self.buf, self.index, self.sends, self.recvs = buf, index, sends, recvs
        self.there, self.partner, self.share = there, partner, share
        self.count = 0
        self.waits = {}
        self.copies = []
        self.shared = []

    def send(self, way, side, step):
        where = self.index(side, step)
        if way == "+":
            name = (side, step + 1)
        elif way == "-":
            name = (side, step - 1)
        else:
            name = ("B", step)
        copy = pltpu.make_async_remote_copy(
            src_ref=self.buf.at[where], dst_ref=self.buf.at[where], send_sem=self.sends.at[self.count],
            recv_sem=self.recvs.at[self.count], device_id=self.there[way], device_id_type=MESH)
        copy.start()
        self.count += 1
        self.copies.append(copy)
        self.waits[name] = copy

    def give(self, side, step):
        if self.share is None:
            return
        where = self.index(side, step)
        n = len(self.shared)
        copy = pltpu.make_async_remote_copy(
            src_ref=self.buf.at[where], dst_ref=self.buf.at[where], send_sem=self.share[0].at[n],
            recv_sem=self.share[1].at[n], device_id=self.partner, device_id_type=MESH)
        copy.start()
        self.shared.append(copy)

    def begin(self):
        for way in "+-s":
            self.send(way, "A", 0)
        self.give("A", 0)

    def take(self, side, step):
        self.waits[side, step].wait_recv()
        for way in self.RELAYS.get((side, step), ""):
            self.send(way, side, step)
        self.give(side, step)


def layer_kernel(
    queries_hbm, keys_hbm, values_hbm, sinks_ref, ow_hbm, gain_ref, routes_t_ref, gates_t_ref,
    gc_hbm, uc_hbm, dc_hbm, gs, us, ds,
    out_ref,
    q_in, kv, qz, bias, sink_rows, heads, wbuf, branch_ref, normed_ref,
    gct, uct, dct, gc, uc, dc, planes, perm, wg, wu, wd,
    send, mine, other, p_mine, p_other, p_in, result, ret,
    in_sem, kv_send, kv_recv, ow_send, ow_recv, give_send, give_recv,
    send_sem, mine_sem, fwd_sem, other_sem, pout_sem, pin_sem, res_sem, ret_sem,
):
    me = lax.axis_index("exp")
    ctx = lax.axis_index("ctx")
    core = me & 1
    z = (me >> 1) & 7
    x_hi = me >> 4
    y = ctx >> 1
    x_lo = ctx & 1

    def peer(i):
        dx, dz = OFFSETS[i]
        return {"exp": (((x_hi + dx) & 1) * 8 + ((z + dz + 8) & 7)) * 2 + core}

    def source(i):
        dx, dz = OFFSETS[i]
        return {"exp": (((x_hi + dx) & 1) * 8 + ((z - dz + 8) & 7)) * 2 + core}

    partner = {"exp": me ^ 1}
    kv_there = {
        "+": {"ctx": ((y + 1) & 7) * 2 + x_lo}, "-": {"ctx": ((y + 7) & 7) * 2 + x_lo}, "s": {"ctx": ctx ^ 1},
    }
    ow_there = {
        "+": {"exp": (x_hi * 8 + ((z + 1) & 7)) * 2 + core}, "-": {"exp": (x_hi * 8 + ((z + 7) & 7)) * 2 + core},
        "s": {"ctx": ctx ^ 1, "exp": me ^ 16},
    }

    def kv_index(side, step):
        return ((y - step + 8) & 7) * 2 + (x_lo if side == "A" else 1 - x_lo)

    def ow_index(side, step):
        return ((x_hi if side == "A" else 1 - x_hi) * 8 + ((z - step + 8) & 7)) * 2 + core

    kv_gather = Gather(kv, kv_index, kv_send, kv_recv, kv_there)
    ow_gather = Gather(wbuf, ow_index, ow_send, ow_recv, ow_there, partner, (give_send, give_recv))

    barrier = pltpu.get_barrier_semaphore()
    greeted = [peer(i) for i in range(1, CHIPS)] + [partner, kv_there["+"], kv_there["-"], kv_there["s"], ow_there["s"]]
    for device in greeted:
        pl.semaphore_signal(barrier, inc=1, device_id=device, device_id_type=MESH)

    loads = []
    for n, (src, dst) in enumerate((
        (keys_hbm, kv.at[ctx, :, 0:256]), (values_hbm, kv.at[ctx, :, 256:512]), (ow_hbm, wbuf.at[me]),
        (gc_hbm, gct), (uc_hbm, uct), (dc_hbm, dct), (queries_hbm, q_in),
    )):
        copy = pltpu.make_async_copy(src, dst, in_sem.at[n])
        copy.start()
        loads.append(copy)
    loads[0].wait()
    loads[1].wait()
    loads[2].wait()
    pl.semaphore_wait(barrier, len(greeted))
    kv_gather.begin()
    ow_gather.begin()

    wide = iota((512, 512), 0)
    perm[:512, :] = (iota((512, 512), 1) == 4 * (wide & 127) + (wide >> 7)).astype(F32).astype(BF16)
    narrow = iota((256, 512), 0)
    perm[512:768, :] = (iota((256, 512), 1) == 4 * (narrow & 63) + (narrow >> 6)).astype(F32).astype(BF16)
    wg[D:, :] = jnp.zeros((DP - D, FF), BF16)
    wu[D:, :] = jnp.zeros((DP - D, FF), BF16)
    wd[:, D:] = jnp.zeros((FF, DP - D), BF16)
    normed_ref[:, D:] = jnp.zeros((TOK, DP - D), BF16)
    loads[3].wait()
    turn(gct, gc, D, 192)
    for name in (("A", 1), ("A", -1), ("B", 0)):
        kv_gather.take(*name)
    code_planes(gc, planes, D, 192)
    for name in (("A", 1), ("A", -1), ("B", 0)):
        ow_gather.take(*name)
    for name in (("A", 2), ("A", -2), ("B", -1)):
        kv_gather.take(*name)
    weight_rows(planes, gs, perm, wg, D, 192, 288)
    for name in (("A", 3), ("A", -3)):
        kv_gather.take(*name)
    loads[4].wait()
    turn(uct, uc, D, 192)
    code_planes(uc, planes, D, 192)
    for name in (("A", 2), ("A", -2), ("B", -1)):
        ow_gather.take(*name)
    kv_gather.take("A", 4)
    weight_rows(planes, us, perm, wu, D, 192, 288)

    loads[6].wait()
    left = iota((TOK, 128), 1) < 64
    for h in range(QH):
        g = h // 8
        tile = q_in[:, 128 * (h // 2) : 128 * (h // 2) + 128].astype(F32) * (1.0 / math.sqrt(HD))
        if h % 2 != g % 2:
            tile = pltpu.roll(tile, 64, 1)
        tile = jnp.where(left if g % 2 == 0 else ~left, tile, 0.0).astype(BF16)
        lo = 128 * (g // 2)
        qz[64 * h : 64 * h + 64, lo : lo + 128] = tile
        qz[64 * h : 64 * h + 64, 128 - lo : 256 - lo] = jnp.zeros((TOK, 128), BF16)
        sink_rows[64 * h : 64 * h + 64, :] = jnp.broadcast_to(sinks_ref[h], (TOK, 128))
    bias[...] = jnp.where(iota((TOK, 1024), 1) <= ctx * TOK + iota((TOK, 1024), 0), 0.0, -1e30)

    for name in (("A", 3), ("A", -3)):
        ow_gather.take(*name)
    loads[5].wait()
    turn(dct, dc, FF, 360)
    code_planes(dc, planes, FF, 360)
    for name in (("B", 1), ("B", -2), ("B", 2), ("B", 3), ("B", -3), ("B", 4)):
        kv_gather.take(*name)

    def attend(i, _):
        r = pl.multiple_of(i * 256, 256)
        scores = lax.dot_general(
            qz[pl.ds(r, 256), :], kv[:, :, 0:256].reshape(1024, 256), (((1,), (1,)), ((), ())),
            preferred_element_type=F32)
        scores = (scores.reshape(4, TOK, 1024) + bias[...][None]).reshape(256, 1024)
        sink = sink_rows[pl.ds(r, 256), :1]
        top = jnp.maximum(jnp.max(scores, axis=1, keepdims=True), sink)
        prob = jnp.exp(scores - top)
        total = jnp.exp(sink - top) + jnp.sum(prob, axis=1, keepdims=True)
        heads[pl.ds(r, 256), :] = dot(prob.astype(BF16), kv[:, :, 256:512].reshape(1024, 256)) / total
        return 0

    lax.fori_loop(0, 4, attend, 0)
    ow_gather.take("A", 4)
    lax.fori_loop(4, 8, attend, 0)
    for name in (("B", 1), ("B", -2), ("B", 2), ("B", 3), ("B", -3), ("B", 4)):
        ow_gather.take(*name)

    tiles = []
    for m in range(QH // 2):
        g = m // 4
        pair = []
        for h in (2 * m, 2 * m + 1):
            tile = heads[64 * h : 64 * h + 64, 128 * (g // 2) : 128 * (g // 2) + 128]
            pair.append(pltpu.roll(tile, 64, 1) if h % 2 != g % 2 else tile)
        tiles.append(jnp.where(left, pair[0], pair[1]).astype(BF16))
    attended = jnp.concatenate(tiles, axis=1)
    for copy in ow_gather.shared:
        copy.wait_recv()
    branch = dot(attended, wbuf[...].reshape(QH * HD, D))
    branch_ref[...] = branch
    mean_sq = jnp.sum(branch * branch, axis=1, keepdims=True) * (1.0 / D)
    normed_ref[:, :D] = (branch * lax.rsqrt(mean_sq + 1e-05) * gain_ref[...].reshape(1, D)).astype(BF16)

    routes_t = routes_t_ref[...]
    expert = offset_expert(iota((CHIPS, TOK), 0), x_hi, z)
    hit = jnp.zeros((CHIPS, TOK), F32)
    for k in range(TOPK):
        hit = hit + (routes_t[k : k + 1, :] == expert).astype(F32)
    before = (iota((TOK, 256), 0) < (iota((TOK, 256), 1) & 63)).astype(BF16)
    same = (iota((TOK, 256), 0) == (iota((TOK, 256), 1) & 63)).astype(BF16)
    hit16 = hit.astype(BF16)
    slot4 = dot(hit16, before)
    hit4 = dot(hit16, same)
    slot4 = jnp.where(hit4 > 0.5, slot4, -1000.0)
    slot_i = slot4.astype(jnp.int32)
    slot_main = slot_i[:, :TOK]
    pick = (jnp.broadcast_to(slot_main[:, None, :], (CHIPS, 16, TOK)) == iota((CHIPS, 16, TOK), 1)).astype(F32)
    pick = pick.astype(BF16).reshape(CHIPS * 16, TOK)
    rows = dot(pick, normed_ref[...]).astype(BF16)
    for j in range(12):
        send[:, 16 * j : 16 * j + 16, :] = rows[:, 128 * j : 128 * j + 128].reshape(CHIPS, 16, 128)
    tail_key = jnp.where(slot_i >= 16, slot_i - 16 + 4 * (iota((CHIPS, 256), 1) >> 6), -1)
    tail = (jnp.broadcast_to(tail_key[:, None, :], (CHIPS, 16, 256)) == iota((CHIPS, 16, 256), 1)).astype(F32)
    tail = tail.astype(BF16).reshape(CHIPS * 16, 256)
    for g in range(3):
        stacked = jnp.concatenate([normed_ref[:, 128 * (4 * g + j) : 128 * (4 * g + j + 1)] for j in range(4)], axis=0)
        send[:, 192 + 16 * g : 208 + 16 * g, :] = dot(tail, stacked).astype(BF16).reshape(CHIPS, 16, 128)

    outgoing = []
    for i in range(1, CHIPS):
        copy = pltpu.make_async_remote_copy(
            src_ref=send.at[i], dst_ref=mine.at[i], send_sem=send_sem.at[i], recv_sem=mine_sem.at[i],
            device_id=peer(i), device_id_type=MESH)
        copy.start()
        outgoing.append(copy)

    def forward(i):
        copy = pltpu.make_async_remote_copy(
            src_ref=send.at[0] if i == 0 else mine.at[i], dst_ref=other.at[i],
            send_sem=fwd_sem.at[i], recv_sem=other_sem.at[i],
            device_id=partner, device_id_type=MESH)
        copy.start()
        return copy

    forwards = [forward(0)]

    padded = jnp.concatenate(
        [routes_t.astype(F32), gates_t_ref[...]], axis=0)
    padded = jnp.transpose(jnp.concatenate([padded, jnp.zeros((8, 64), F32)], axis=1))[:TOK, :]
    routes = padded[:, :TOPK].astype(jnp.int32)
    gates = padded[:, TOPK:]
    expert_of = offset_expert(iota((TOK, CHIPS), 1), x_hi, z)
    hits = jnp.zeros((TOK, CHIPS), F32)
    for k in range(TOPK):
        hits = hits + (routes[:, k : k + 1] == expert_of).astype(F32)
    earlier = (iota((TOK, TOK), 1) < iota((TOK, TOK), 0)).astype(BF16)
    slots = jnp.where(hits > 0.5, dot(earlier, hits.astype(BF16)), 100.0)
    spread = (iota((CHIPS, 256), 0) == (iota((CHIPS, 256), 1) >> 4)).astype(BF16)
    slots = dot(slots.astype(BF16), spread).astype(jnp.int32)
    column_expert = offset_expert(iota((TOK, 256), 1) >> 4, x_hi, z)
    weight = jnp.zeros((TOK, 256), F32)
    for k in range(TOPK):
        weight = weight + jnp.where(routes[:, k : k + 1] == column_expert, gates[:, k : k + 1], 0.0)
    place = iota((TOK, 256), 1) & 15
    combine_main = jnp.concatenate(split3(jnp.where(slots == place, weight, 0.0)), axis=0)
    combine_tail = [
        jnp.concatenate(split3(jnp.where((slots - 16 == (place & 3)) & ((place >> 2) == j), weight, 0.0)), axis=0)
        for j in range(4)
    ]

    weight_rows(planes, ds, perm, wd, FF, 360, 256)

    a, b = iota((128, 128), 0), iota((128, 128), 1)
    to_rows = (b == ((a >> 2) & 7) * 16 + (a >> 5) * 4 + (a & 3)).astype(F32).astype(BF16)
    to_block = (a == ((b >> 2) & 7) * 16 + (b >> 5) * 4 + (b & 3)).astype(F32).astype(BF16)

    sent_pieces = []
    sent_results = []

    def finish(c):
        sent_pieces[c].wait_recv()
        for i in range(4 * c, 4 * c + 4):
            total = (p_mine[i].astype(F32) + p_in[i].astype(F32)).astype(BF16)
            if i == 0:
                ret[0] = total
            else:
                result[i] = total
        for i in range(max(1, 4 * c), 4 * c + 4):
            copy = pltpu.make_async_remote_copy(
                src_ref=result.at[i], dst_ref=ret.at[i], send_sem=res_sem.at[i], recv_sem=ret_sem.at[i],
                device_id=source(i), device_id_type=MESH)
            copy.start()
            sent_results.append(copy)

    for c in range(4):
        for i in range(max(1, 4 * c), 4 * c + 4):
            outgoing[i - 1].wait_recv()
            forwards.append(forward(i))
        for i in range(4 * c, 4 * c + 4):
            forwards[i].wait_recv()
        if c == 0:
            mine[0] = send[0]

        def both(lo, hi):
            return jnp.concatenate(
                [mine[4 * c : 4 * c + 4, lo:hi, :].reshape(64, 128), other[4 * c : 4 * c + 4, lo:hi, :].reshape(64, 128)],
                axis=0)

        main = jnp.concatenate([both(16 * j, 16 * j + 16) for j in range(12)], axis=1)
        tails = []
        for g in range(3):
            moved = dot(to_rows, both(192 + 16 * g, 208 + 16 * g)).astype(BF16)
            tails += [moved[32 * j : 32 * j + 32, :] for j in range(4)]
        x = jnp.concatenate([main, jnp.concatenate(tails, axis=1)], axis=0)
        gate_act = dot(x, wg[...])
        up_act = dot(x, wu[...])
        active = ((up_act + 1.0) * gate_act * jax.nn.sigmoid(1.702 * gate_act)).astype(BF16)
        y = dot(active, wd[...]).astype(BF16)
        for j in range(12):
            tile = y[:128, 128 * j : 128 * j + 128]
            p_mine[4 * c : 4 * c + 4, 16 * j : 16 * j + 16, :] = tile[:64].reshape(4, 16, 128)
            p_other[4 * c : 4 * c + 4, 16 * j : 16 * j + 16, :] = tile[64:].reshape(4, 16, 128)
        for g in range(3):
            tiles = jnp.concatenate([y[128:, 128 * (4 * g + j) : 128 * (4 * g + j + 1)] for j in range(4)], axis=0)
            back = dot(to_block, tiles).astype(BF16)
            p_mine[4 * c : 4 * c + 4, 192 + 16 * g : 208 + 16 * g, :] = back[:64].reshape(4, 16, 128)
            p_other[4 * c : 4 * c + 4, 192 + 16 * g : 208 + 16 * g, :] = back[64:].reshape(4, 16, 128)
        copy = pltpu.make_async_remote_copy(
            src_ref=p_other.at[pl.ds(4 * c, 4)], dst_ref=p_in.at[pl.ds(4 * c, 4)],
            send_sem=pout_sem.at[c], recv_sem=pin_sem.at[c], device_id=partner, device_id_type=MESH)
        copy.start()
        sent_pieces.append(copy)
        if c > 0:
            finish(c - 1)
    finish(3)

    for copy in sent_results:
        copy.wait_recv()
    for j in range(12):
        part = dot(combine_main, ret[:, 16 * j : 16 * j + 16, :].reshape(256, 128))
        g = j // 4
        part = part + dot(combine_tail[j % 4], ret[:, 192 + 16 * g : 208 + 16 * g, :].reshape(256, 128))
        mixed = part[:TOK] + part[TOK : 2 * TOK] + part[2 * TOK :]
        lo, hi = 128 * j, min(128 * j + 128, D)
        out_ref[:, lo:hi] = (branch_ref[:, lo:hi] + mixed[:, : hi - lo]).astype(BF16)

    for copy in outgoing + forwards + sent_pieces + sent_results + kv_gather.copies + ow_gather.copies + ow_gather.shared:
        copy.wait_send()


def local(
    queries, keys, values, sinks, out_weight, norm_gain, routes, gates,
    gate_codes, up_codes, down_codes, gate_scales, up_scales, down_scales,
):
    vmem = pl.BlockSpec(memory_space=pltpu.VMEM)
    hbm = pl.BlockSpec(memory_space=pl.ANY)
    dma = pltpu.SemaphoreType.DMA
    blocks = pltpu.VMEM((CHIPS, BLK, 128), BF16)
    out = pl.pallas_call(
        layer_kernel,
        out_shape=jax.ShapeDtypeStruct((TOK, D), BF16),
        in_specs=[hbm] * 3 + [pl.BlockSpec(memory_space=pltpu.SMEM), hbm] + [vmem] * 3 + [hbm] * 3 + [vmem] * 3,
        out_specs=vmem,
        scratch_shapes=[
            pltpu.VMEM((TOK, QH * HD), BF16),
            pltpu.VMEM((16, TOK, 512), BF16),
            pltpu.VMEM((QH * TOK, 256), BF16),
            pltpu.VMEM((TOK, 1024), F32),
            pltpu.VMEM((QH * TOK, 128), F32),
            pltpu.VMEM((QH * TOK, 256), F32),
            pltpu.VMEM((32, 64, D), BF16),
            pltpu.VMEM((TOK, D), F32),
            pltpu.VMEM((TOK, DP), BF16),
            pltpu.VMEM((192, D), jnp.int32),
            pltpu.VMEM((192, D), jnp.int32),
            pltpu.VMEM((360, FF), jnp.int32),
            pltpu.VMEM((D, 192), jnp.int32),
            pltpu.VMEM((D, 192), jnp.int32),
            pltpu.VMEM((FF, 360), jnp.int32),
            pltpu.VMEM((D, DP), BF16),
            pltpu.VMEM((FF, 512), BF16),
            pltpu.VMEM((DP, FF), BF16),
            pltpu.VMEM((DP, FF), BF16),
            pltpu.VMEM((FF, DP), BF16),
            blocks, blocks, blocks, blocks, blocks, blocks, blocks, blocks,
            dma((7,)), dma((15,)), dma((15,)), dma((15,)), dma((15,)), dma((16,)), dma((16,)),
            dma((CHIPS,)), dma((CHIPS,)), dma((CHIPS,)), dma((CHIPS,)), dma((4,)), dma((4,)),
            dma((CHIPS,)), dma((CHIPS,)),
        ],
        compiler_params=pltpu.CompilerParams(collective_id=0, has_side_effects=True, vmem_limit_bytes=60 * 1024 * 1024),
        name="layer",
    )(
        queries[0], keys[0], values[0], sinks, out_weight, norm_gain.reshape(1, D), routes[0].T, gates[0].T,
        gate_codes[0].T, up_codes[0].T, down_codes[0].T, gate_scales[0], up_scales[0], down_scales[0],
    )
    return out[None]


def solution(mesh):
    return jax.shard_map(
        local,
        mesh=mesh,
        in_specs=(
            P("exp", "ctx", None),
            P("exp", "ctx", None),
            P("exp", "ctx", None),
            P(),
            P("exp", None),
            P(),
            P("exp", "ctx", None),
            P("exp", "ctx", None),
            P("exp", None, None),
            P("exp", None, None),
            P("exp", None, None),
            P("exp", None, None),
            P("exp", None, None),
            P("exp", None, None),
        ),
        out_specs=P("exp", "ctx", None),
        check_vma=False,
    )
```

time: 192 us -> 114 us (0.59)
  blocking collectives: 58 us -> 0 us
  Pallas kernels: 58.1 us -> 109 us
  waiting for transfers between devices: 41 us -> 0 us
  between operations: 13.6 us -> 0.01 us
  local copies, waits for them, and re-layouts: 12.4 us -> 4.61 us
  matrix products: 5.17 us -> 0 us
    all_gather x2 -> x0, blocking collectives: 58 us -> none  [the longest x1 31.5 us: local(): lax.all_gather(keys[0], 'ctx', axis=0, tiled=True)]
    pallas_call x1, Pallas kernels: 58.1 us -> 109 us  [local(): pl.pallas_call(layer_kernel, out_shape=jax.ShapeDtypeStruct((TOK, D), BF1...]
    all_gather x1 -> x0, waiting for transfers between devices: 40.3 us -> none  [local(): lax.all_gather(out_weight, 'exp', axis=0, tiled=True)]
    dot_general x3 -> x0, matrix products: 5.17 us -> none  [the longest x1 4.06 us: local(): jnp.dot(attended, lax.all_gather(out_weight, 'exp', axis=0, tiled=True),...]
    unnamed x30 -> x2, local copies, waits for them, and re-layouts: 7.63 us -> 3.32 us
    another operation x3 -> x0, local copies, waits for them, and re-layouts: 2 us -> none  [the longest x1 0.75 us: moe(): gate_scales.reshape(5, 9, FF)]
  transfers between devices with their start and end apart: 1 -> 0, of which waited for: 1 -> 0; matrix products, arithmetic and copies ran while one was open for 7% -> 0% of each run, Pallas kernels for 0% -> 0%
where the time goes in v2:
time: 114 us
  Pallas kernels  109 us (96%)
  local copies, waits for them, and re-layouts  4.61 us (4%)
    pallas_call x1, Pallas kernels, local(): pl.pallas_call(layer_kernel, out_shape=jax.ShapeDtypeStruct((TOK, D), BF1...  109 us
    unnamed x2, local copies, waits for them, and re-layouts  3.32 us

profile of v2, /device:TPU:1, one launch (start us, length us, event | category | flops | bytes accessed | tf_op | source)
XLA Modules:
  0.0 113.8 jit_solution(4547585681051096250)
XLA Ops:
  0.0 1.3 %reshape.3.gain_ref = f32[1,1440]{1,0:T(1,128)} reshape(f32[1440]{0:T(1024)} %param.19) | data formatting | bytes 11520 | tf_op jit(solution)/shard_map/reshape | solution.py:501
  1.3 1.7 %copy_bitcast_fusion = (s32[45,768]{1,0:T(8,128)}, s32[45,768]{1,0:T(8,128)}) fusion(s32[1,45,768]{2,0,1:T(1,128)} %param.26, s32[1,45,768]{2,0,1:T(1,128)} %param.25), kind=kLoop, calls=%fused_computation | loop fusion | bytes 552960
  3.0 109.2 %layer.1 = bf16[64,1440]{1,0:T(8,128)(2,1)} custom-call(bf16[64,2048]{1,0:T(8,128)(2,1)} %bitcast.28, bf16[64,256]{1,0:T(8,128)(2,1)} %bitcast.30, bf16[64,256]{1,0:T(8,128)(2,1)} %bitcast.31, f32[32]{0:T(128)} %sinks_ref.1, bf16[64,1440]{1,0:T(8,128)(2,1)} %ow_hbm.1, f32[1,1440]{1,0:T(1,128)} %reshape.3.gain_ref, s32[4,64]{1,0:T(4,128)} %bitcast.32, ...), custom_call_target="tpu_custom_call" | custom-call | tf_op jit(solution)/shard_map/layer/pallas_call | solution.py:467
  112.2 1.6 %copy.20 = bf16[1,64,1440]{2,1,0:T(8,128)(2,1)} copy(bf16[1,64,1440]{2,1,0:T(8,128)(2,1)} %bitcast.27) | data formatting | bytes 368640

commit v3 on v2

--- a/solution.py
+++ b/solution.py
@@ -99,10 +99,10 @@
             else:
                 value = dot(planes_ref[r : r + m_rows, 512 * b : 512 * b + 512], perm_ref[:512, :])
             value = value[:, :width]
-            scale = scales_ref[groups * i : groups * (i + 1), 512 * b : 512 * b + width]
+            scale = scales_ref[groups * i : groups * (i + 1), ..., 512 * b : 512 * b + width]
             factor = (1 << (scale - 118)).astype(F32) * (2.0**-10)
             for n in range(groups):
-                piece = value[32 * n : 32 * n + 32] * factor[n : n + 1]
+                piece = value[32 * n : 32 * n + 32] * (factor[n] if factor.ndim == 3 else factor[n : n + 1])
                 out_ref[r + 32 * n : r + 32 * n + 32, 512 * b : 512 * b + width] = piece.astype(BF16)
 
 
@@ -113,13 +113,12 @@
         ("B", 0): "+-", ("B", -1): "-",
     }
 
-    def __init__(self, buf, index, sends, recvs, there, partner=None, share=None):
+    def __init__(self, buf, index, sends, recvs, there):
         self.buf, self.index, self.sends, self.recvs = buf, index, sends, recvs
-        self.there, self.partner, self.share = there, partner, share
+        self.there = there
         self.count = 0
         self.waits = {}
         self.copies = []
-        self.shared = []
 
     def send(self, way, side, step):
         where = self.index(side, step)
@@ -137,34 +136,82 @@
         self.copies.append(copy)
         self.waits[name] = copy
 
-    def give(self, side, step):
-        if self.share is None:
-            return
-        where = self.index(side, step)
-        n = len(self.shared)
-        copy = pltpu.make_async_remote_copy(
-            src_ref=self.buf.at[where], dst_ref=self.buf.at[where], send_sem=self.share[0].at[n],
-            recv_sem=self.share[1].at[n], device_id=self.partner, device_id_type=MESH)
-        copy.start()
-        self.shared.append(copy)
-
     def begin(self):
         for way in "+-s":
             self.send(way, "A", 0)
-        self.give("A", 0)
 
     def take(self, side, step):
         self.waits[side, step].wait_recv()
         for way in self.RELAYS.get((side, step), ""):
             self.send(way, side, step)
-        self.give(side, step)
+
+
+class WeightGather:
+    def __init__(self, buf, unit, turn, there, partner, sems):
+        self.buf, self.unit, self.sign, self.there, self.partner = buf, unit, turn, there, partner
+        self.sends, self.recvs, self.give_sends, self.give_recvs = sems
+        self.copies, self.given, self.by_name = [], [], {}
+
+    def send(self, name, way, side, step, half):
+        where = self.unit(side, step, half)
+        n = len(self.copies)
+        copy = pltpu.make_async_remote_copy(
+            src_ref=self.buf.at[where], dst_ref=self.buf.at[where], send_sem=self.sends.at[n],
+            recv_sem=self.recvs.at[n], device_id=self.there[way], device_id_type=MESH)
+        copy.start()
+        self.copies.append(copy)
+        self.by_name[name + (half,)] = copy
+
+    def give(self, side, step, half):
+        where = self.unit(side, step, half)
+        n = len(self.given)
+        copy = pltpu.make_async_remote_copy(
+            src_ref=self.buf.at[where], dst_ref=self.buf.at[where], send_sem=self.give_sends.at[n],
+            recv_sem=self.give_recvs.at[n], device_id=self.partner, device_id_type=MESH)
+        copy.start()
+        self.given.append(copy)
+
+    def begin(self):
+        for half in range(2):
+            self.send(("A", 1), "+", "A", 0, half)
+            self.send(("A", -1), "-", "A", 0, half)
+            self.send(("B", 0), "cross", "A", 0, half)
+        for half in range(2):
+            self.give("A", 0, half)
+
+    def ring(self, k, half):
+        ways = [1, -1] if k < 4 else [1 if half == 0 else -1]
+        for way in ways:
+            self.by_name["A", way * k, half].wait_recv()
+        for way in ways:
+            if k < 3 or (k == 3 and (half == 0) == (way == 1)):
+                self.send(("A", way * (k + 1)), "+" if way == 1 else "-", "A", way * k, half)
+        if k < 4:
+            self.send(("B", "near", k), "cross", "A", -self.sign * k, half)
+        else:
+            self.send(("B", 4), "cross", "A", 4, half)
+        for way in ways:
+            self.give("A", way * k, half)
+
+    def near(self, k, half):
+        self.by_name["B", "near", k, half].wait_recv()
+        self.send(("B", "far", k), "pair", "B", self.sign * k, half)
+        self.give("B", self.sign * k, half)
+
+    def far(self, k, half):
+        self.by_name["B", "far", k, half].wait_recv()
+        self.give("B", -self.sign * k, half)
+
+    def other(self, k, half):
+        self.by_name["B", k, half].wait_recv()
+        self.give("B", k, half)
 
 
 def layer_kernel(
     queries_hbm, keys_hbm, values_hbm, sinks_ref, ow_hbm, gain_ref, routes_t_ref, gates_t_ref,
     gc_hbm, uc_hbm, dc_hbm, gs, us, ds,
     out_ref,
-    q_in, kv, qz, bias, sink_rows, heads, wbuf, branch_ref, normed_ref,
+    q_in, kv, qz, tops, totals, heads, wbuf, branch_ref, normed_ref,
     gct, uct, dct, gc, uc, dc, planes, perm, wg, wu, wd,
     send, mine, other, p_mine, p_other, p_in, result, ret,
     in_sem, kv_send, kv_recv, ow_send, ow_recv, give_send, give_recv,
@@ -180,11 +227,11 @@
 
     def peer(i):
         dx, dz = OFFSETS[i]
-        return {"exp": (((x_hi + dx) & 1) * 8 + ((z + dz + 8) & 7)) * 2 + core}
+        return {"exp": (((x_hi + dx) & 1) * 8 + ((z + dz + 8) & 7)) * 2 + core, "ctx": ctx ^ dx}
 
     def source(i):
         dx, dz = OFFSETS[i]
-        return {"exp": (((x_hi + dx) & 1) * 8 + ((z - dz + 8) & 7)) * 2 + core}
+        return {"exp": (((x_hi + dx) & 1) * 8 + ((z - dz + 8) & 7)) * 2 + core, "ctx": ctx ^ dx}
 
     partner = {"exp": me ^ 1}
     kv_there = {
@@ -192,26 +239,27 @@
     }
     ow_there = {
         "+": {"exp": (x_hi * 8 + ((z + 1) & 7)) * 2 + core}, "-": {"exp": (x_hi * 8 + ((z + 7) & 7)) * 2 + core},
-        "s": {"ctx": ctx ^ 1, "exp": me ^ 16},
+        "cross": {"ctx": ctx ^ 1, "exp": me ^ 16}, "pair": {"ctx": ctx ^ 1},
     }
 
     def kv_index(side, step):
         return ((y - step + 8) & 7) * 2 + (x_lo if side == "A" else 1 - x_lo)
 
-    def ow_index(side, step):
-        return ((x_hi if side == "A" else 1 - x_hi) * 8 + ((z - step + 8) & 7)) * 2 + core
+    def ow_unit(side, step, half):
+        return (((x_hi if side == "A" else 1 - x_hi) * 8 + ((z - step + 8) & 7)) * 2 + core) * 2 + half
 
     kv_gather = Gather(kv, kv_index, kv_send, kv_recv, kv_there)
-    ow_gather = Gather(wbuf, ow_index, ow_send, ow_recv, ow_there, partner, (give_send, give_recv))
+    ow_gather = WeightGather(
+        wbuf, ow_unit, 1 - 2 * x_lo, ow_there, partner, (ow_send, ow_recv, give_send, give_recv))
 
     barrier = pltpu.get_barrier_semaphore()
-    greeted = [peer(i) for i in range(1, CHIPS)] + [partner, kv_there["+"], kv_there["-"], kv_there["s"], ow_there["s"]]
+    greeted = [peer(i) for i in range(1, CHIPS)] + [partner, kv_there["+"], kv_there["-"], kv_there["s"]]
     for device in greeted:
         pl.semaphore_signal(barrier, inc=1, device_id=device, device_id_type=MESH)
 
     loads = []
     for n, (src, dst) in enumerate((
-        (keys_hbm, kv.at[ctx, :, 0:256]), (values_hbm, kv.at[ctx, :, 256:512]), (ow_hbm, wbuf.at[me]),
+        (keys_hbm, kv.at[ctx, :, 0:256]), (values_hbm, kv.at[ctx, :, 256:512]), (ow_hbm, wbuf.at[pl.ds(2 * me, 2)]),
         (gc_hbm, gct), (uc_hbm, uct), (dc_hbm, dct), (queries_hbm, q_in),
     )):
         copy = pltpu.make_async_copy(src, dst, in_sem.at[n])
@@ -224,34 +272,6 @@
     kv_gather.begin()
     ow_gather.begin()
 
-    wide = iota((512, 512), 0)
-    perm[:512, :] = (iota((512, 512), 1) == 4 * (wide & 127) + (wide >> 7)).astype(F32).astype(BF16)
-    narrow = iota((256, 512), 0)
-    perm[512:768, :] = (iota((256, 512), 1) == 4 * (narrow & 63) + (narrow >> 6)).astype(F32).astype(BF16)
-    wg[D:, :] = jnp.zeros((DP - D, FF), BF16)
-    wu[D:, :] = jnp.zeros((DP - D, FF), BF16)
-    wd[:, D:] = jnp.zeros((FF, DP - D), BF16)
-    normed_ref[:, D:] = jnp.zeros((TOK, DP - D), BF16)
-    loads[3].wait()
-    turn(gct, gc, D, 192)
-    for name in (("A", 1), ("A", -1), ("B", 0)):
-        kv_gather.take(*name)
-    code_planes(gc, planes, D, 192)
-    for name in (("A", 1), ("A", -1), ("B", 0)):
-        ow_gather.take(*name)
-    for name in (("A", 2), ("A", -2), ("B", -1)):
-        kv_gather.take(*name)
-    weight_rows(planes, gs, perm, wg, D, 192, 288)
-    for name in (("A", 3), ("A", -3)):
-        kv_gather.take(*name)
-    loads[4].wait()
-    turn(uct, uc, D, 192)
-    code_planes(uc, planes, D, 192)
-    for name in (("A", 2), ("A", -2), ("B", -1)):
-        ow_gather.take(*name)
-    kv_gather.take("A", 4)
-    weight_rows(planes, us, perm, wu, D, 192, 288)
-
     loads[6].wait()
     left = iota((TOK, 128), 1) < 64
     for h in range(QH):
@@ -263,35 +283,83 @@
         lo = 128 * (g // 2)
         qz[64 * h : 64 * h + 64, lo : lo + 128] = tile
         qz[64 * h : 64 * h + 64, 128 - lo : 256 - lo] = jnp.zeros((TOK, 128), BF16)
-        sink_rows[64 * h : 64 * h + 64, :] = jnp.broadcast_to(sinks_ref[h], (TOK, 128))
-    bias[...] = jnp.where(iota((TOK, 1024), 1) <= ctx * TOK + iota((TOK, 1024), 0), 0.0, -1e30)
-
-    for name in (("A", 3), ("A", -3)):
-        ow_gather.take(*name)
-    loads[5].wait()
-    turn(dct, dc, FF, 360)
-    code_planes(dc, planes, FF, 360)
-    for name in (("B", 1), ("B", -2), ("B", 2), ("B", 3), ("B", -3), ("B", 4)):
-        kv_gather.take(*name)
-
-    def attend(i, _):
-        r = pl.multiple_of(i * 256, 256)
-        scores = lax.dot_general(
-            qz[pl.ds(r, 256), :], kv[:, :, 0:256].reshape(1024, 256), (((1,), (1,)), ((), ())),
-            preferred_element_type=F32)
-        scores = (scores.reshape(4, TOK, 1024) + bias[...][None]).reshape(256, 1024)
-        sink = sink_rows[pl.ds(r, 256), :1]
-        top = jnp.maximum(jnp.max(scores, axis=1, keepdims=True), sink)
-        prob = jnp.exp(scores - top)
-        total = jnp.exp(sink - top) + jnp.sum(prob, axis=1, keepdims=True)
-        heads[pl.ds(r, 256), :] = dot(prob.astype(BF16), kv[:, :, 256:512].reshape(1024, 256)) / total
-        return 0
-
-    lax.fori_loop(0, 4, attend, 0)
-    ow_gather.take("A", 4)
-    lax.fori_loop(4, 8, attend, 0)
-    for name in (("B", 1), ("B", -2), ("B", 2), ("B", 3), ("B", -3), ("B", 4)):
-        ow_gather.take(*name)
+        tops[64 * h : 64 * h + 64, :] = jnp.broadcast_to(sinks_ref[h], (TOK, 128))
+    normed_ref[:, D:] = jnp.zeros((TOK, DP - D), BF16)
+
+    def attend(names, part, first=False):
+        where = [kv_index(*name) for name in names]
+        lane = iota((TOK, 256), 1)
+        owner = jnp.where(lane < 128, jnp.where(lane < 64, where[0], where[1]), jnp.where(lane < 192, where[2], where[3]))
+        bias = jnp.where(owner * TOK + (lane & 63) <= ctx * TOK + iota((TOK, 256), 0), 0.0, -1e30)
+
+        def rows(i, _):
+            r = pl.multiple_of(i * 512, 512)
+            key_block = jnp.concatenate([kv[w, :, 0:256] for w in where], axis=0)
+            value_block = jnp.concatenate([kv[w, :, 256:512] for w in where], axis=0)
+            scores = lax.dot_general(
+                qz[pl.ds(r, 512), :], key_block, (((1,), (1,)), ((), ())), preferred_element_type=F32)
+            scores = (scores.reshape(8, TOK, 256) + bias[None]).reshape(512, 256)
+            old = tops[pl.ds(r, 512), :1]
+            top = jnp.maximum(jnp.max(scores, axis=1, keepdims=True), old)
+            prob = jnp.exp(scores - top)
+            shrink = jnp.exp(old - top)
+            added = jnp.sum(prob, axis=1, keepdims=True)
+            value = dot(prob.astype(BF16), value_block)
+            tops[pl.ds(r, 512), :] = jnp.broadcast_to(top, (512, 128))
+            if first:
+                totals[pl.ds(r, 512), :] = jnp.broadcast_to(shrink + added, (512, 128))
+                heads[pl.ds(r, 512), :] = value
+            else:
+                totals[pl.ds(r, 512), :] = totals[pl.ds(r, 512), :] * shrink + added
+                heads[pl.ds(r, 512), :] = heads[pl.ds(r, 512), :] * shrink + value
+            return 0
+
+        lax.fori_loop(2 * part, 2 * part + 2, rows, 0)
+
+    def take(*names):
+        for name in names:
+            kv_gather.take(*name)
+
+    chunks = [
+        (("A", 0), ("A", 1), ("A", -1), ("B", 0)), (("A", 2), ("A", -2), ("B", 1), ("B", -1)),
+        (("A", 3), ("A", -3), ("B", 2), ("B", -2)), (("A", 4), ("B", 3), ("B", -3), ("B", 4)),
+    ]
+    take(*chunks[0][1:])
+    ow_gather.ring(1, 0)
+    attend(chunks[0], 0, True)
+    ow_gather.ring(1, 1)
+    take(("A", 2), ("A", -2))
+    attend(chunks[0], 1, True)
+    take(("B", 1), ("B", -1))
+    ow_gather.ring(2, 0)
+    take(("A", 3), ("A", -3))
+    ow_gather.near(1, 0)
+    ow_gather.near(1, 1)
+    attend(chunks[1], 0)
+    ow_gather.ring(2, 1)
+    take(("B", 2), ("B", -2))
+    attend(chunks[1], 1)
+    take(("A", 4),)
+    ow_gather.ring(3, 0)
+    ow_gather.near(2, 0)
+    attend(chunks[2], 0)
+    ow_gather.near(2, 1)
+    attend(chunks[2], 1)
+    ow_gather.ring(3, 1)
+    take(("B", 3), ("B", -3), ("B", 4))
+    ow_gather.near(3, 0)
+    attend(chunks[3], 0)
+    ow_gather.ring(4, 0)
+    ow_gather.ring(4, 1)
+    attend(chunks[3], 1)
+    ow_gather.near(3, 1)
+    ow_gather.other(0, 0)
+    ow_gather.other(0, 1)
+    loads[3].wait()
+    turn(gct, gc, D, 192)
+    for k in (1, 2):
+        for half in range(2):
+            ow_gather.far(k, half)
 
     tiles = []
     for m in range(QH // 2):
@@ -299,10 +367,14 @@
         pair = []
         for h in (2 * m, 2 * m + 1):
             tile = heads[64 * h : 64 * h + 64, 128 * (g // 2) : 128 * (g // 2) + 128]
+            tile = tile / totals[64 * h : 64 * h + 64, :]
             pair.append(pltpu.roll(tile, 64, 1) if h % 2 != g % 2 else tile)
         tiles.append(jnp.where(left, pair[0], pair[1]).astype(BF16))
     attended = jnp.concatenate(tiles, axis=1)
-    for copy in ow_gather.shared:
+    for half in range(2):
+        ow_gather.far(3, half)
+        ow_gather.other(4, half)
+    for copy in ow_gather.given:
         copy.wait_recv()
     branch = dot(attended, wbuf[...].reshape(QH * HD, D))
     branch_ref[...] = branch
@@ -376,6 +448,22 @@
         for j in range(4)
     ]
 
+    wide = iota((512, 512), 0)
+    perm[:512, :] = (iota((512, 512), 1) == 4 * (wide & 127) + (wide >> 7)).astype(F32).astype(BF16)
+    narrow = iota((256, 512), 0)
+    perm[512:768, :] = (iota((256, 512), 1) == 4 * (narrow & 63) + (narrow >> 6)).astype(F32).astype(BF16)
+    wg[D:, :] = jnp.zeros((DP - D, FF), BF16)
+    wu[D:, :] = jnp.zeros((DP - D, FF), BF16)
+    wd[:, D:] = jnp.zeros((FF, DP - D), BF16)
+    code_planes(gc, planes, D, 192)
+    weight_rows(planes, gs, perm, wg, D, 192, 288)
+    loads[4].wait()
+    turn(uct, uc, D, 192)
+    code_planes(uc, planes, D, 192)
+    weight_rows(planes, us, perm, wu, D, 192, 288)
+    loads[5].wait()
+    turn(dct, dc, FF, 360)
+    code_planes(dc, planes, FF, 360)
     weight_rows(planes, ds, perm, wd, FF, 360, 256)
 
     a, b = iota((128, 128), 0), iota((128, 128), 1)
@@ -450,9 +538,9 @@
         part = part + dot(combine_tail[j % 4], ret[:, 192 + 16 * g : 208 + 16 * g, :].reshape(256, 128))
         mixed = part[:TOK] + part[TOK : 2 * TOK] + part[2 * TOK :]
         lo, hi = 128 * j, min(128 * j + 128, D)
-        out_ref[:, lo:hi] = (branch_ref[:, lo:hi] + mixed[:, : hi - lo]).astype(BF16)
-
-    for copy in outgoing + forwards + sent_pieces + sent_results + kv_gather.copies + ow_gather.copies + ow_gather.shared:
+        out_ref[:, lo:hi] = branch_ref[:, lo:hi] + mixed[:, : hi - lo]
+
+    for copy in outgoing + forwards + sent_pieces + sent_results + kv_gather.copies + ow_gather.copies + ow_gather.given:
         copy.wait_send()
 
 
@@ -466,17 +554,17 @@
     blocks = pltpu.VMEM((CHIPS, BLK, 128), BF16)
     out = pl.pallas_call(
         layer_kernel,
-        out_shape=jax.ShapeDtypeStruct((TOK, D), BF16),
+        out_shape=jax.ShapeDtypeStruct((TOK, D), F32),
         in_specs=[hbm] * 3 + [pl.BlockSpec(memory_space=pltpu.SMEM), hbm] + [vmem] * 3 + [hbm] * 3 + [vmem] * 3,
         out_specs=vmem,
         scratch_shapes=[
             pltpu.VMEM((TOK, QH * HD), BF16),
             pltpu.VMEM((16, TOK, 512), BF16),
             pltpu.VMEM((QH * TOK, 256), BF16),
-            pltpu.VMEM((TOK, 1024), F32),
+            pltpu.VMEM((QH * TOK, 128), F32),
             pltpu.VMEM((QH * TOK, 128), F32),
             pltpu.VMEM((QH * TOK, 256), F32),
-            pltpu.VMEM((32, 64, D), BF16),
+            pltpu.VMEM((64, 32, D), BF16),
             pltpu.VMEM((TOK, D), F32),
             pltpu.VMEM((TOK, DP), BF16),
             pltpu.VMEM((192, D), jnp.int32),
@@ -491,17 +579,17 @@
             pltpu.VMEM((DP, FF), BF16),
             pltpu.VMEM((FF, DP), BF16),
             blocks, blocks, blocks, blocks, blocks, blocks, blocks, blocks,
-            dma((7,)), dma((15,)), dma((15,)), dma((15,)), dma((15,)), dma((16,)), dma((16,)),
+            dma((7,)), dma((15,)), dma((15,)), dma((30,)), dma((30,)), dma((32,)), dma((32,)),
             dma((CHIPS,)), dma((CHIPS,)), dma((CHIPS,)), dma((CHIPS,)), dma((4,)), dma((4,)),
             dma((CHIPS,)), dma((CHIPS,)),
         ],
         compiler_params=pltpu.CompilerParams(collective_id=0, has_side_effects=True, vmem_limit_bytes=60 * 1024 * 1024),
         name="layer",
     )(
-        queries[0], keys[0], values[0], sinks, out_weight, norm_gain.reshape(1, D), routes[0].T, gates[0].T,
-        gate_codes[0].T, up_codes[0].T, down_codes[0].T, gate_scales[0], up_scales[0], down_scales[0],
+        queries[0], keys[0], values[0], sinks, out_weight.reshape(2, 32, D), norm_gain, routes[0].T, gates[0].T,
+        gate_codes[0].T, up_codes[0].T, down_codes[0].T, jnp.swapaxes(gate_scales, 0, 1), jnp.swapaxes(up_scales, 0, 1), down_scales[0],
     )
-    return out[None]
+    return out.astype(BF16)[None]
 
 
 def solution(mesh):

time: 114 us -> 108 us (0.947); the launches traced: 114 us -> 106 us
  Pallas kernels: 109 us -> 104 us
  local copies, waits for them, and re-layouts: 4.61 us -> 0 us
  other arithmetic: 0 us -> 1.69 us
    pallas_call x1, Pallas kernels: 109 us -> 104 us  [local(): pl.pallas_call(layer_kernel, out_shape=jax.ShapeDtypeStruct((TOK, D), F32...]
    unnamed x2 -> x0, local copies, waits for them, and re-layouts: 3.32 us -> none
    broadcast_in_dim x0 -> x1, other arithmetic: none -> 1.69 us  [local(): return out.astype(BF16)[None]]
    reshape x1 -> x0, local copies, waits for them, and re-layouts: 1.29 us -> none  [local(): norm_gain.reshape(1, D)]
where the time goes in v3:
time: 108 us; the launch traced here: 106 us
  Pallas kernels  104 us (96%)
  other arithmetic  1.69 us (2%)
    pallas_call x1, Pallas kernels, local(): pl.pallas_call(layer_kernel, out_shape=jax.ShapeDtypeStruct((TOK, D), F32...  104 us

profile of v3, /device:TPU:1, one launch (start us, length us, event | category | flops | bytes accessed | tf_op | source)
XLA Modules:
  0.0 105.5 jit_solution(4150952520983250410)
XLA Ops:
  0.0 103.8 %layer.1 = f32[64,1440]{1,0:T(8,128)} custom-call(bf16[64,2048]{1,0:T(8,128)(2,1)} %bitcast.27, bf16[64,256]{1,0:T(8,128)(2,1)} %bitcast.32, bf16[64,256]{1,0:T(8,128)(2,1)} %bitcast.33, f32[32]{0:T(128)} %sinks_ref.1, bf16[2,32,1440]{2,1,0:T(8,128)(2,1)} %bitcast.28, f32[1440]{0:T(1024)} %gain_ref.1, s32[4,64]{1,0:T(4,128)} %bitcast.34, f32[4,64]{1,0:T(4,128)} %bitcast.35, ...), custom_call_target="tpu_custom_call" | custom-call | tf_op jit(solution)/shard_map/layer/pallas_call | solution.py:555
  103.8 1.7 %convert_bitcast_fusion = bf16[1,64,1440]{2,1,0:T(8,128)(2,1)} fusion(f32[64,1440]{1,0:T(8,128)} %layer.1), kind=kLoop, calls=%fused_computation | loop fusion | flops 92160 | bytes 552960 | tf_op jit(solution)/shard_map/broadcast_in_dim | solution.py:592

commit v4 on v3

--- a/solution.py
+++ b/solution.py
@@ -150,7 +150,7 @@
     def __init__(self, buf, unit, turn, there, partner, sems):
         self.buf, self.unit, self.sign, self.there, self.partner = buf, unit, turn, there, partner
         self.sends, self.recvs, self.give_sends, self.give_recvs = sems
-        self.copies, self.given, self.by_name = [], [], {}
+        self.copies, self.given, self.by_name, self.given_by = [], [], {}, {}
 
     def send(self, name, way, side, step, half):
         where = self.unit(side, step, half)
@@ -162,7 +162,7 @@
         self.copies.append(copy)
         self.by_name[name + (half,)] = copy
 
-    def give(self, side, step, half):
+    def give(self, name, side, step, half):
         where = self.unit(side, step, half)
         n = len(self.given)
         copy = pltpu.make_async_remote_copy(
@@ -170,6 +170,7 @@
             recv_sem=self.give_recvs.at[n], device_id=self.partner, device_id_type=MESH)
         copy.start()
         self.given.append(copy)
+        self.given_by[name] = self.given_by.get(name, []) + [copy]
 
     def begin(self):
         for half in range(2):
@@ -177,7 +178,7 @@
             self.send(("A", -1), "-", "A", 0, half)
             self.send(("B", 0), "cross", "A", 0, half)
         for half in range(2):
-            self.give("A", 0, half)
+            self.give(("A", 0), "A", 0, half)
 
     def ring(self, k, half):
         ways = [1, -1] if k < 4 else [1 if half == 0 else -1]
@@ -191,27 +192,27 @@
         else:
             self.send(("B", 4), "cross", "A", 4, half)
         for way in ways:
-            self.give("A", way * k, half)
+            self.give(("A", way * k if k < 4 else 4), "A", way * k, half)
 
     def near(self, k, half):
         self.by_name["B", "near", k, half].wait_recv()
         self.send(("B", "far", k), "pair", "B", self.sign * k, half)
-        self.give("B", self.sign * k, half)
+        self.give(("near", k), "B", self.sign * k, half)
 
     def far(self, k, half):
         self.by_name["B", "far", k, half].wait_recv()
-        self.give("B", -self.sign * k, half)
+        self.give(("far", k), "B", -self.sign * k, half)
 
     def other(self, k, half):
         self.by_name["B", k, half].wait_recv()
-        self.give("B", k, half)
+        self.give(("B", k), "B", k, half)
 
 
 def layer_kernel(
     queries_hbm, keys_hbm, values_hbm, sinks_ref, ow_hbm, gain_ref, routes_t_ref, gates_t_ref,
     gc_hbm, uc_hbm, dc_hbm, gs, us, ds,
     out_ref,
-    q_in, kv, qz, tops, totals, heads, wbuf, branch_ref, normed_ref,
+    q_in, kv, qz, tops, totals, heads, attended, wbuf, branch_ref, normed_ref,
     gct, uct, dct, gc, uc, dc, planes, perm, wg, wu, wd,
     send, mine, other, p_mine, p_other, p_in, result, ret,
     in_sem, kv_send, kv_recv, ow_send, ow_recv, give_send, give_recv,
@@ -330,6 +331,8 @@
     ow_gather.ring(1, 1)
     take(("A", 2), ("A", -2))
     attend(chunks[0], 1, True)
+    ow_gather.other(0, 0)
+    ow_gather.other(0, 1)
     take(("B", 1), ("B", -1))
     ow_gather.ring(2, 0)
     take(("A", 3), ("A", -3))
@@ -345,6 +348,8 @@
     attend(chunks[2], 0)
     ow_gather.near(2, 1)
     attend(chunks[2], 1)
+    ow_gather.far(1, 0)
+    ow_gather.far(1, 1)
     ow_gather.ring(3, 1)
     take(("B", 3), ("B", -3), ("B", 4))
     ow_gather.near(3, 0)
@@ -353,15 +358,9 @@
     ow_gather.ring(4, 1)
     attend(chunks[3], 1)
     ow_gather.near(3, 1)
-    ow_gather.other(0, 0)
-    ow_gather.other(0, 1)
-    loads[3].wait()
-    turn(gct, gc, D, 192)
-    for k in (1, 2):
-        for half in range(2):
-            ow_gather.far(k, half)
-
-    tiles = []
+    for half in range(2):
+        ow_gather.far(2, half)
+
     for m in range(QH // 2):
         g = m // 4
         pair = []
@@ -369,14 +368,26 @@
             tile = heads[64 * h : 64 * h + 64, 128 * (g // 2) : 128 * (g // 2) + 128]
             tile = tile / totals[64 * h : 64 * h + 64, :]
             pair.append(pltpu.roll(tile, 64, 1) if h % 2 != g % 2 else tile)
-        tiles.append(jnp.where(left, pair[0], pair[1]).astype(BF16))
-    attended = jnp.concatenate(tiles, axis=1)
+        attended[m] = jnp.where(left, pair[0], pair[1]).astype(BF16)
+
+    def project(blocks):
+        chips = [(x_hi if side == "A" else 1 - x_hi) * 8 + ((z - step + 8) & 7) for side, step in blocks]
+        return dot(
+            jnp.concatenate([attended[m] for m in chips], axis=1),
+            jnp.concatenate([wbuf[pl.ds(4 * m, 4)].reshape(128, D) for m in chips], axis=0))
+
+    for name in (("A", 0), ("A", 1), ("A", -1), ("A", 2), ("A", -2), ("B", 0), ("near", 1), ("far", 1)):
+        for copy in ow_gather.given_by[name]:
+            copy.wait_recv()
+    branch = project([("A", 0), ("A", 1), ("A", -1), ("A", 2), ("A", -2), ("B", 0), ("B", 1), ("B", -1)])
     for half in range(2):
         ow_gather.far(3, half)
         ow_gather.other(4, half)
-    for copy in ow_gather.given:
-        copy.wait_recv()
-    branch = dot(attended, wbuf[...].reshape(QH * HD, D))
+    for name in (("A", 3), ("A", -3), ("A", 4), ("near", 2), ("far", 2), ("near", 3), ("far", 3), ("B", 4)):
+        for copy in ow_gather.given_by[name]:
+            copy.wait_recv()
+    branch = branch + project(
+        [("A", 3), ("A", -3), ("A", 4), ("B", 2), ("B", -2), ("B", 3), ("B", -3), ("B", 4)])
     branch_ref[...] = branch
     mean_sq = jnp.sum(branch * branch, axis=1, keepdims=True) * (1.0 / D)
     normed_ref[:, :D] = (branch * lax.rsqrt(mean_sq + 1e-05) * gain_ref[...].reshape(1, D)).astype(BF16)
@@ -406,13 +417,13 @@
         stacked = jnp.concatenate([normed_ref[:, 128 * (4 * g + j) : 128 * (4 * g + j + 1)] for j in range(4)], axis=0)
         send[:, 192 + 16 * g : 208 + 16 * g, :] = dot(tail, stacked).astype(BF16).reshape(CHIPS, 16, 128)
 
-    outgoing = []
-    for i in range(1, CHIPS):
+    outgoing = {}
+    for i in reversed(range(1, CHIPS)):
         copy = pltpu.make_async_remote_copy(
             src_ref=send.at[i], dst_ref=mine.at[i], send_sem=send_sem.at[i], recv_sem=mine_sem.at[i],
             device_id=peer(i), device_id_type=MESH)
         copy.start()
-        outgoing.append(copy)
+        outgoing[i] = copy
 
     def forward(i):
         copy = pltpu.make_async_remote_copy(
@@ -422,7 +433,7 @@
         copy.start()
         return copy
 
-    forwards = [forward(0)]
+    forwards = {0: forward(0)}
 
     padded = jnp.concatenate(
         [routes_t.astype(F32), gates_t_ref[...]], axis=0)
@@ -455,6 +466,8 @@
     wg[D:, :] = jnp.zeros((DP - D, FF), BF16)
     wu[D:, :] = jnp.zeros((DP - D, FF), BF16)
     wd[:, D:] = jnp.zeros((FF, DP - D), BF16)
+    loads[3].wait()
+    turn(gct, gc, D, 192)
     code_planes(gc, planes, D, 192)
     weight_rows(planes, gs, perm, wg, D, 192, 288)
     loads[4].wait()
@@ -470,8 +483,9 @@
     to_rows = (b == ((a >> 2) & 7) * 16 + (a >> 5) * 4 + (a & 3)).astype(F32).astype(BF16)
     to_block = (a == ((b >> 2) & 7) * 16 + (b >> 5) * 4 + (b & 3)).astype(F32).astype(BF16)
 
-    sent_pieces = []
+    sent_pieces = {}
     sent_results = []
+    done = []
 
     def finish(c):
         sent_pieces[c].wait_recv()
@@ -481,17 +495,17 @@
                 ret[0] = total
             else:
                 result[i] = total
-        for i in range(max(1, 4 * c), 4 * c + 4):
+        for i in reversed(range(max(1, 4 * c), 4 * c + 4)):
             copy = pltpu.make_async_remote_copy(
                 src_ref=result.at[i], dst_ref=ret.at[i], send_sem=res_sem.at[i], recv_sem=ret_sem.at[i],
                 device_id=source(i), device_id_type=MESH)
             copy.start()
             sent_results.append(copy)
 
-    for c in range(4):
-        for i in range(max(1, 4 * c), 4 * c + 4):
-            outgoing[i - 1].wait_recv()
-            forwards.append(forward(i))
+    for c in (3, 2, 1, 0):
+        for i in reversed(range(max(1, 4 * c), 4 * c + 4)):
+            outgoing[i].wait_recv()
+            forwards[i] = forward(i)
         for i in range(4 * c, 4 * c + 4):
             forwards[i].wait_recv()
         if c == 0:
@@ -525,10 +539,11 @@
             src_ref=p_other.at[pl.ds(4 * c, 4)], dst_ref=p_in.at[pl.ds(4 * c, 4)],
             send_sem=pout_sem.at[c], recv_sem=pin_sem.at[c], device_id=partner, device_id_type=MESH)
         copy.start()
-        sent_pieces.append(copy)
-        if c > 0:
-            finish(c - 1)
-    finish(3)
+        sent_pieces[c] = copy
+        if done:
+            finish(done[-1])
+        done.append(c)
+    finish(0)
 
     for copy in sent_results:
         copy.wait_recv()
@@ -540,7 +555,7 @@
         lo, hi = 128 * j, min(128 * j + 128, D)
         out_ref[:, lo:hi] = branch_ref[:, lo:hi] + mixed[:, : hi - lo]
 
-    for copy in outgoing + forwards + sent_pieces + sent_results + kv_gather.copies + ow_gather.copies + ow_gather.given:
+    for copy in list(outgoing.values()) + list(forwards.values()) + list(sent_pieces.values()) + sent_results + kv_gather.copies + ow_gather.copies + ow_gather.given:
         copy.wait_send()
 
 
@@ -564,6 +579,7 @@
             pltpu.VMEM((QH * TOK, 128), F32),
             pltpu.VMEM((QH * TOK, 128), F32),
             pltpu.VMEM((QH * TOK, 256), F32),
+            pltpu.VMEM((QH // 2, TOK, 128), BF16),
             pltpu.VMEM((64, 32, D), BF16),
             pltpu.VMEM((TOK, D), F32),
             pltpu.VMEM((TOK, DP), BF16),

time: 108 us -> 105 us (0.972); the launches traced: 106 us -> 105 us
  no operation moved by 1% of the time
where the time goes in v4:
time: 105 us
  Pallas kernels  103 us (98%)
  other arithmetic  1.69 us (2%)
    pallas_call x1, Pallas kernels, local(): pl.pallas_call(layer_kernel, out_shape=jax.ShapeDtypeStruct((TOK, D), F32...  103 us

profile of v4, /device:TPU:1, one launch (start us, length us, event | category | flops | bytes accessed | tf_op | source)
XLA Modules:
  0.0 104.9 jit_solution(7670183538703909201)
XLA Ops:
  0.0 103.2 %layer.1 = f32[64,1440]{1,0:T(8,128)} custom-call(bf16[64,2048]{1,0:T(8,128)(2,1)} %bitcast.27, bf16[64,256]{1,0:T(8,128)(2,1)} %bitcast.32, bf16[64,256]{1,0:T(8,128)(2,1)} %bitcast.33, f32[32]{0:T(128)} %sinks_ref.1, bf16[2,32,1440]{2,1,0:T(8,128)(2,1)} %bitcast.28, f32[1440]{0:T(1024)} %gain_ref.1, s32[4,64]{1,0:T(4,128)} %bitcast.34, f32[4,64]{1,0:T(4,128)} %bitcast.35, ...), custom_call_target="tpu_custom_call" | custom-call | tf_op jit(solution)/shard_map/layer/pallas_call | solution.py:570
  103.2 1.7 %convert_bitcast_fusion = bf16[1,64,1440]{2,1,0:T(8,128)(2,1)} fusion(f32[64,1440]{1,0:T(8,128)} %layer.1), kind=kLoop, calls=%fused_computation | loop fusion | flops 92160 | bytes 552960 | tf_op jit(solution)/shard_map/broadcast_in_dim | solution.py:608

commit v5 on v4

--- a/solution.py
+++ b/solution.py
@@ -18,6 +18,7 @@
 TOK = 64
 CHIPS = 16
 BLK = 240
+GROUP = 4
 MESH = pl.DeviceIdType.MESH
 F32 = jnp.float32
 BF16 = jnp.bfloat16
@@ -435,6 +436,12 @@
 
     forwards = {0: forward(0)}
 
+    def arrive(c):
+        for i in reversed(range(max(1, GROUP * c), GROUP * (c + 1))):
+            outgoing[i].wait_recv()
+            forwards[i] = forward(i)
+
+
     padded = jnp.concatenate(
         [routes_t.astype(F32), gates_t_ref[...]], axis=0)
     padded = jnp.transpose(jnp.concatenate([padded, jnp.zeros((8, 64), F32)], axis=1))[:TOK, :]
@@ -477,73 +484,71 @@
     loads[5].wait()
     turn(dct, dc, FF, 360)
     code_planes(dc, planes, FF, 360)
+    arrive(CHIPS // GROUP - 1)
     weight_rows(planes, ds, perm, wd, FF, 360, 256)
 
-    a, b = iota((128, 128), 0), iota((128, 128), 1)
-    to_rows = (b == ((a >> 2) & 7) * 16 + (a >> 5) * 4 + (a & 3)).astype(F32).astype(BF16)
-    to_block = (a == ((b >> 2) & 7) * 16 + (b >> 5) * 4 + (b & 3)).astype(F32).astype(BF16)
+    side = 32 * GROUP
+    a, b = iota((side, side), 0), iota((side, side), 1)
+    moved_to = lambda r: ((r >> 2) % (2 * GROUP)) * 16 + (r // (8 * GROUP)) * 4 + (r & 3)
+    to_rows = (b == moved_to(a)).astype(F32).astype(BF16)
+    to_block = (a == moved_to(b)).astype(F32).astype(BF16)
 
     sent_pieces = {}
     sent_results = []
-    done = []
 
     def finish(c):
         sent_pieces[c].wait_recv()
-        for i in range(4 * c, 4 * c + 4):
+        for i in range(GROUP * c, GROUP * (c + 1)):
             total = (p_mine[i].astype(F32) + p_in[i].astype(F32)).astype(BF16)
             if i == 0:
                 ret[0] = total
             else:
                 result[i] = total
-        for i in reversed(range(max(1, 4 * c), 4 * c + 4)):
+        for i in reversed(range(max(1, GROUP * c), GROUP * (c + 1))):
             copy = pltpu.make_async_remote_copy(
                 src_ref=result.at[i], dst_ref=ret.at[i], send_sem=res_sem.at[i], recv_sem=ret_sem.at[i],
                 device_id=source(i), device_id_type=MESH)
             copy.start()
             sent_results.append(copy)
 
-    for c in (3, 2, 1, 0):
-        for i in reversed(range(max(1, 4 * c), 4 * c + 4)):
-            outgoing[i].wait_recv()
-            forwards[i] = forward(i)
-        for i in range(4 * c, 4 * c + 4):
+    for c in reversed(range(CHIPS // GROUP)):
+        if c < CHIPS // GROUP - 1:
+            arrive(c)
+        for i in range(GROUP * c, GROUP * (c + 1)):
             forwards[i].wait_recv()
         if c == 0:
             mine[0] = send[0]
 
         def both(lo, hi):
             return jnp.concatenate(
-                [mine[4 * c : 4 * c + 4, lo:hi, :].reshape(64, 128), other[4 * c : 4 * c + 4, lo:hi, :].reshape(64, 128)],
+                [ref[GROUP * c : GROUP * (c + 1), lo:hi, :].reshape(16 * GROUP, 128) for ref in (mine, other)],
                 axis=0)
 
         main = jnp.concatenate([both(16 * j, 16 * j + 16) for j in range(12)], axis=1)
         tails = []
         for g in range(3):
             moved = dot(to_rows, both(192 + 16 * g, 208 + 16 * g)).astype(BF16)
-            tails += [moved[32 * j : 32 * j + 32, :] for j in range(4)]
+            tails += [moved[8 * GROUP * j : 8 * GROUP * (j + 1), :] for j in range(4)]
         x = jnp.concatenate([main, jnp.concatenate(tails, axis=1)], axis=0)
         gate_act = dot(x, wg[...])
         up_act = dot(x, wu[...])
         active = ((up_act + 1.0) * gate_act * jax.nn.sigmoid(1.702 * gate_act)).astype(BF16)
         y = dot(active, wd[...]).astype(BF16)
         for j in range(12):
-            tile = y[:128, 128 * j : 128 * j + 128]
-            p_mine[4 * c : 4 * c + 4, 16 * j : 16 * j + 16, :] = tile[:64].reshape(4, 16, 128)
-            p_other[4 * c : 4 * c + 4, 16 * j : 16 * j + 16, :] = tile[64:].reshape(4, 16, 128)
+            tile = y[:side, 128 * j : 128 * j + 128]
+            p_mine[GROUP * c : GROUP * (c + 1), 16 * j : 16 * j + 16, :] = tile[: side // 2].reshape(GROUP, 16, 128)
+            p_other[GROUP * c : GROUP * (c + 1), 16 * j : 16 * j + 16, :] = tile[side // 2 :].reshape(GROUP, 16, 128)
         for g in range(3):
-            tiles = jnp.concatenate([y[128:, 128 * (4 * g + j) : 128 * (4 * g + j + 1)] for j in range(4)], axis=0)
+            tiles = jnp.concatenate([y[side:, 128 * (4 * g + j) : 128 * (4 * g + j + 1)] for j in range(4)], axis=0)
             back = dot(to_block, tiles).astype(BF16)
-            p_mine[4 * c : 4 * c + 4, 192 + 16 * g : 208 + 16 * g, :] = back[:64].reshape(4, 16, 128)
-            p_other[4 * c : 4 * c + 4, 192 + 16 * g : 208 + 16 * g, :] = back[64:].reshape(4, 16, 128)
+            p_mine[GROUP * c : GROUP * (c + 1), 192 + 16 * g : 208 + 16 * g, :] = back[: side // 2].reshape(GROUP, 16, 128)
+            p_other[GROUP * c : GROUP * (c + 1), 192 + 16 * g : 208 + 16 * g, :] = back[side // 2 :].reshape(GROUP, 16, 128)
         copy = pltpu.make_async_remote_copy(
-            src_ref=p_other.at[pl.ds(4 * c, 4)], dst_ref=p_in.at[pl.ds(4 * c, 4)],
+            src_ref=p_other.at[pl.ds(GROUP * c, GROUP)], dst_ref=p_in.at[pl.ds(GROUP * c, GROUP)],
             send_sem=pout_sem.at[c], recv_sem=pin_sem.at[c], device_id=partner, device_id_type=MESH)
         copy.start()
         sent_pieces[c] = copy
-        if done:
-            finish(done[-1])
-        done.append(c)
-    finish(0)
+        finish(c)
 
     for copy in sent_results:
         copy.wait_recv()
@@ -596,7 +601,7 @@
             pltpu.VMEM((FF, DP), BF16),
             blocks, blocks, blocks, blocks, blocks, blocks, blocks, blocks,
             dma((7,)), dma((15,)), dma((15,)), dma((30,)), dma((30,)), dma((32,)), dma((32,)),
-            dma((CHIPS,)), dma((CHIPS,)), dma((CHIPS,)), dma((CHIPS,)), dma((4,)), dma((4,)),
+            dma((CHIPS,)), dma((CHIPS,)), dma((CHIPS,)), dma((CHIPS,)), dma((CHIPS // GROUP,)), dma((CHIPS // GROUP,)),
             dma((CHIPS,)), dma((CHIPS,)),
         ],
         compiler_params=pltpu.CompilerParams(collective_id=0, has_side_effects=True, vmem_limit_bytes=60 * 1024 * 1024),

time: 105 us -> 102 us (0.971)
  Pallas kernels: 103 us -> 101 us
    pallas_call x1, Pallas kernels: 103 us -> 101 us  [local(): pl.pallas_call(layer_kernel, out_shape=jax.ShapeDtypeStruct((TOK, D), F32...]
where the time goes in v5:
time: 102 us
  Pallas kernels  101 us (99%)
  other arithmetic  1.69 us (2%)
    pallas_call x1, Pallas kernels, local(): pl.pallas_call(layer_kernel, out_shape=jax.ShapeDtypeStruct((TOK, D), F32...  101 us

profile of v5, /device:TPU:1, one launch (start us, length us, event | category | flops | bytes accessed | tf_op | source)
XLA Modules:
  0.0 102.2 jit_solution(1928387763700634989)
XLA Ops:
  0.0 100.5 %layer.1 = f32[64,1440]{1,0:T(8,128)} custom-call(bf16[64,2048]{1,0:T(8,128)(2,1)} %bitcast.27, bf16[64,256]{1,0:T(8,128)(2,1)} %bitcast.32, bf16[64,256]{1,0:T(8,128)(2,1)} %bitcast.33, f32[32]{0:T(128)} %sinks_ref.1, bf16[2,32,1440]{2,1,0:T(8,128)(2,1)} %bitcast.28, f32[1440]{0:T(1024)} %gain_ref.1, s32[4,64]{1,0:T(4,128)} %bitcast.34, f32[4,64]{1,0:T(4,128)} %bitcast.35, ...), custom_call_target="tpu_custom_call" | custom-call | tf_op jit(solution)/shard_map/layer/pallas_call | solution.py:575
  100.5 1.7 %convert_bitcast_fusion = bf16[1,64,1440]{2,1,0:T(8,128)(2,1)} fusion(f32[64,1440]{1,0:T(8,128)} %layer.1), kind=kLoop, calls=%fused_computation | loop fusion | flops 92160 | bytes 552960 | tf_op jit(solution)/shard_map/broadcast_in_dim | solution.py:613

commit v6 on v5

--- a/solution.py
+++ b/solution.py
@@ -377,6 +377,25 @@
             jnp.concatenate([attended[m] for m in chips], axis=1),
             jnp.concatenate([wbuf[pl.ds(4 * m, 4)].reshape(128, D) for m in chips], axis=0))
 
+    routes_t = routes_t_ref[...]
+    expert = offset_expert(iota((CHIPS, TOK), 0), x_hi, z)
+    hit = jnp.zeros((CHIPS, TOK), F32)
+    for k in range(TOPK):
+        hit = hit + (routes_t[k : k + 1, :] == expert).astype(F32)
+    before = (iota((TOK, 256), 0) < (iota((TOK, 256), 1) & 63)).astype(BF16)
+    same = (iota((TOK, 256), 0) == (iota((TOK, 256), 1) & 63)).astype(BF16)
+    hit16 = hit.astype(BF16)
+    slot4 = dot(hit16, before)
+    hit4 = dot(hit16, same)
+    slot4 = jnp.where(hit4 > 0.5, slot4, -1000.0)
+    slot_i = slot4.astype(jnp.int32)
+    slot_main = slot_i[:, :TOK]
+    pick = (jnp.broadcast_to(slot_main[:, None, :], (CHIPS, 16, TOK)) == iota((CHIPS, 16, TOK), 1)).astype(F32)
+    pick = pick.astype(BF16).reshape(CHIPS * 16, TOK)
+    tail_key = jnp.where(slot_i >= 16, slot_i - 16 + 4 * (iota((CHIPS, 256), 1) >> 6), -1)
+    tail = (jnp.broadcast_to(tail_key[:, None, :], (CHIPS, 16, 256)) == iota((CHIPS, 16, 256), 1)).astype(F32)
+    tail = tail.astype(BF16).reshape(CHIPS * 16, 256)
+
     for name in (("A", 0), ("A", 1), ("A", -1), ("A", 2), ("A", -2), ("B", 0), ("near", 1), ("far", 1)):
         for copy in ow_gather.given_by[name]:
             copy.wait_recv()
@@ -393,27 +412,9 @@
     mean_sq = jnp.sum(branch * branch, axis=1, keepdims=True) * (1.0 / D)
     normed_ref[:, :D] = (branch * lax.rsqrt(mean_sq + 1e-05) * gain_ref[...].reshape(1, D)).astype(BF16)
 
-    routes_t = routes_t_ref[...]
-    expert = offset_expert(iota((CHIPS, TOK), 0), x_hi, z)
-    hit = jnp.zeros((CHIPS, TOK), F32)
-    for k in range(TOPK):
-        hit = hit + (routes_t[k : k + 1, :] == expert).astype(F32)
-    before = (iota((TOK, 256), 0) < (iota((TOK, 256), 1) & 63)).astype(BF16)
-    same = (iota((TOK, 256), 0) == (iota((TOK, 256), 1) & 63)).astype(BF16)
-    hit16 = hit.astype(BF16)
-    slot4 = dot(hit16, before)
-    hit4 = dot(hit16, same)
-    slot4 = jnp.where(hit4 > 0.5, slot4, -1000.0)
-    slot_i = slot4.astype(jnp.int32)
-    slot_main = slot_i[:, :TOK]
-    pick = (jnp.broadcast_to(slot_main[:, None, :], (CHIPS, 16, TOK)) == iota((CHIPS, 16, TOK), 1)).astype(F32)
-    pick = pick.astype(BF16).reshape(CHIPS * 16, TOK)
     rows = dot(pick, normed_ref[...]).astype(BF16)
     for j in range(12):
         send[:, 16 * j : 16 * j + 16, :] = rows[:, 128 * j : 128 * j + 128].reshape(CHIPS, 16, 128)
-    tail_key = jnp.where(slot_i >= 16, slot_i - 16 + 4 * (iota((CHIPS, 256), 1) >> 6), -1)
-    tail = (jnp.broadcast_to(tail_key[:, None, :], (CHIPS, 16, 256)) == iota((CHIPS, 16, 256), 1)).astype(F32)
-    tail = tail.astype(BF16).reshape(CHIPS * 16, 256)
     for g in range(3):
         stacked = jnp.concatenate([normed_ref[:, 128 * (4 * g + j) : 128 * (4 * g + j + 1)] for j in range(4)], axis=0)
         send[:, 192 + 16 * g : 208 + 16 * g, :] = dot(tail, stacked).astype(BF16).reshape(CHIPS, 16, 128)

time: 102 us -> 102 us (level)
  no operation moved by 1% of the time
where the time goes in v6:
time: 102 us
  Pallas kernels  100 us (98%)
  other arithmetic  1.69 us (2%)
    pallas_call x1, Pallas kernels, local(): pl.pallas_call(layer_kernel, out_shape=jax.ShapeDtypeStruct((TOK, D), F32...  100 us

profile of v6, /device:TPU:1, one launch (start us, length us, event | category | flops | bytes accessed | tf_op | source)
XLA Modules:
  0.0 102.2 jit_solution(12708862199012369805)
XLA Ops:
  0.0 100.5 %layer.1 = f32[64,1440]{1,0:T(8,128)} custom-call(bf16[64,2048]{1,0:T(8,128)(2,1)} %bitcast.27, bf16[64,256]{1,0:T(8,128)(2,1)} %bitcast.32, bf16[64,256]{1,0:T(8,128)(2,1)} %bitcast.33, f32[32]{0:T(128)} %sinks_ref.1, bf16[2,32,1440]{2,1,0:T(8,128)(2,1)} %bitcast.28, f32[1440]{0:T(1024)} %gain_ref.1, s32[4,64]{1,0:T(4,128)} %bitcast.34, f32[4,64]{1,0:T(4,128)} %bitcast.35, ...), custom_call_target="tpu_custom_call" | custom-call | tf_op jit(solution)/shard_map/layer/pallas_call | solution.py:576
  100.5 1.7 %convert_bitcast_fusion = bf16[1,64,1440]{2,1,0:T(8,128)(2,1)} fusion(f32[64,1440]{1,0:T(8,128)} %layer.1), kind=kLoop, calls=%fused_computation | loop fusion | flops 92160 | bytes 552960 | tf_op jit(solution)/shard_map/broadcast_in_dim | solution.py:614
